TPU v7x, 32 devices: a whole 2x2x4 slice. The times are simulated.
32 devices in a mesh: space: 4 (over z), energy: 8 (over y, x, core).
Axes of the slice: x: 2, y: 2, z: 4, core: 2. Of those that a mesh axis runs over, the one named last changes fastest.
Arguments:
- onsite: float32 [16, 4, 128], P('energy', 'space'), parts along dimension 0, may hold values from -0.8 to 0.8, as said below
- hopping: float32 [16, 4, 128, 128], P('energy', 'space'), parts along dimension 0, may hold values from -0.25 to 0.25, as said below
- coupling: float32 [16, 4, 128, 128], P('energy', 'space'), parts along dimension 0, may hold values from -0.25 to 0.75
Outputs:
- retarded: float32 [16, 4, 128, 128], P('energy', 'space'), parts along dimension 0
There are 8 independent parts, one for each index of `energy`. A program takes and returns all parts, laid end to end along the dimension named above; each array names one. Nothing has to cross between parts.
Inputs may be any that keep to these rules, and one draw needn't show every extreme that they name: Row 1 of onsite (the imaginary parts) lies between 0.002 and 0.01. Every slab's block is Hermitian: hopping[0, k] is symmetric and hopping[1, k] antisymmetric in the last two dimensions.
All inputs are finite; a program needn't handle non-finite values.
Results may differ from a plain program's by a relative error of at most 0.0014.
Values sent between devices are 32-bit elements; how exact they have to be, the bound alone decides.
No kernel may reach another device: no remote copies, remote signals or barrier semaphores. Data moves between devices by JAX's collectives and lax.ppermute only.
A program may use at most 64 MiB of HBM per device.

v0:
```python
import jax
import jax.numpy as jnp
from jax import lax
from jax.sharding import PartitionSpec as P


def from_behind(value, axis, steps):
    count = lax.axis_size(axis)
    first, last = (max(0, -steps), min(count, count - steps))
    return lax.ppermute(value, axis, [(source, source + steps) for source in range(first, last)])


def matmul_exact(former, latter):
    return jnp.matmul(former, latter, precision=lax.Precision.HIGHEST)


def complex_product(former, latter):
    real_part = matmul_exact(former[0], latter[0]) - matmul_exact(former[1], latter[1])
    imaginary = matmul_exact(former[0], latter[1]) + matmul_exact(former[1], latter[0])
    return jnp.stack([real_part, imaginary])


def adjoint(matrix):
    return jnp.stack([matrix[0].T, -matrix[1].T])


def complex_unit(orbitals, scale_real, scale_imag):
    unit = jnp.eye(orbitals, dtype=jnp.float32)
    return jnp.stack([scale_real * unit, scale_imag * unit])


def invert(matrix):
    orbitals = matrix.shape[-1]
    embedded = jnp.concatenate(
        [jnp.concatenate([matrix[0], -matrix[1]], 1), jnp.concatenate([matrix[1], matrix[0]], 1)], 0
    )
    normal = matmul_exact(embedded.T, embedded)
    factor = jnp.linalg.cholesky(normal)
    middle = lax.linalg.triangular_solve(factor, embedded.T, left_side=True, lower=True)
    solved = lax.linalg.triangular_solve(
        factor, middle, left_side=True, lower=True, transpose_a=True
    )
    estimate = jnp.stack([solved[:orbitals, :orbitals], solved[orbitals:, :orbitals]])
    for refine in range(2):
        estimate = complex_product(
            estimate, complex_unit(orbitals, 2.0, 0.0) - complex_product(matrix, estimate)
        )
    return estimate


def forward_sweep(blocks, links, previous):

    def advance(carry, item):
        slab_block, slab_link = item
        matrix = slab_block - complex_product(adjoint(slab_link), complex_product(carry, slab_link))
        fresh = invert(matrix)
        return (fresh, (fresh, matrix))

    _, outputs = lax.scan(advance, previous, (blocks, links))
    return (outputs[0], outputs[1][-1])


def finish(stack, last_matrix, sigma_right, links):
    closing = invert(last_matrix - sigma_right)

    def recede(later_green, item):
        left_green, slab_link = item
        outward = complex_product(left_green, slab_link)
        inward = complex_product(adjoint(slab_link), left_green)
        full = left_green + complex_product(outward, complex_product(later_green, inward))
        return (full, full)

    _, earlier = lax.scan(recede, closing, (stack[:-1], links[1:]), reverse=True)
    return jnp.moveaxis(jnp.concatenate([earlier, closing[None]], 0), 1, 0)


def on_device(onsite, hopping, coupling):
    orbitals = onsite.shape[-1]
    diagonal = jax.vmap(jnp.diag)
    blocks = jnp.stack([diagonal(onsite[0]) - hopping[0], diagonal(onsite[1]) - hopping[1]], 1)
    links = jnp.moveaxis(coupling, 0, 1)
    position = lax.axis_index("space")
    devices = lax.axis_size("space")
    nothing = complex_unit(orbitals, 0.0, 0.0)
    contact = complex_unit(orbitals, 0.0, -1.0)
    empty_stack = jnp.zeros_like(blocks)

    def keep_carry(incoming, carry):
        return carry

    def forward_work(incoming, carry):
        stack, last_matrix = forward_sweep(blocks, links, incoming)
        return (stack[-1], stack, last_matrix)

    forward_start = lax.cond(
        position == 0, forward_work, keep_carry, contact, (nothing, empty_stack, nothing)
    )

    def forward_turn(turn_index, carry):
        incoming = from_behind(carry[0], "space", 1)
        return lax.cond(position == turn_index, forward_work, keep_carry, incoming, carry)

    forward_final = lax.fori_loop(1, devices, forward_turn, forward_start)
    stack = forward_final[1]
    last_matrix = forward_final[2]

    def backward_work(incoming, carry):

        def retreat(sigma, item):
            slab_block, slab_link = item
            right_green = invert(slab_block - sigma)
            return (
                complex_product(slab_link, complex_product(right_green, adjoint(slab_link))),
                None,
            )

        message, _ = lax.scan(retreat, incoming, (blocks, links), reverse=True)
        return (message, incoming)

    backward_start = lax.cond(
        position == devices - 1, backward_work, keep_carry, nothing, (nothing, nothing)
    )

    def backward_turn(turn_index, carry):
        incoming = from_behind(carry[0], "space", -1)
        return lax.cond(
            position == devices - 1 - turn_index, backward_work, keep_carry, incoming, carry
        )

    backward_final = lax.fori_loop(1, devices, backward_turn, backward_start)
    sigma_right = backward_final[1]
    return finish(stack, last_matrix, sigma_right, links)


def solution(mesh):
    return jax.shard_map(
        on_device,
        mesh=mesh,
        in_specs=(
            P("energy", "space", None),
            P("energy", "space", None, None),
            P("energy", "space", None, None),
        ),
        out_specs=P("energy", "space", None, None),
        check_vma=False,
    )
```

profile of v0, /device:TPU:0, one launch (start us, length us, event | category | flops | bytes accessed | tf_op | source)
XLA Modules:
  0.0 655.4 jit_solution(10250436997972073681)
XLA Ops:
  0.0 0.7 slice_bitcast_fusion.133
  0.7 1.0 slice_subtract_fusion.11
  1.7 0.8 copy-done
  2.6 69.5 %conditional.4 = (f32[2,128,128]{2,1,0:T(8,128)S(1)}, f32[1,2,128,128]{3,2,1,0:T(8,128)S(1)}, f32[2,128,128]{1,2,0:T(8,128)S(1)}) conditional(s32[]{:T(128)} %convert_element_type.36, f32[2,128,128]{2,1,0:T(8,128)S(1)} %stack.276, (f32[1,2,128,128]{3,2,1,0:T(8,128)S(1)}, f32[1,2,128,128]{3,2,1,0:T(8,128)S(1)}, pred[1,128,128]{2,1,0:T(32,128)(4,1)S(1)}, ...), branch_computations={%region_0.1_spmd, %region_1.0_spmd} | conditional | flops 1083752448 | bytes 14651671 | solution.py:95
  4.4 0.4 fusion.10
  5.0 11.7 %cholesky.256 = f32[128,128]{1,0:T(8,128)S(1)} custom-call(f32[128,128]{1,0:T(8,128)S(1)} %cholesky.422), custom_call_target="Cholesky" | custom-call | tf_op jit(solution)/shard_map/cond/branch_1_fun/while/body/eval_jaxpr/jit(cholesky)/cholesky | solution.py:38
  16.8 9.8 %custom-call.26 = f32[1,128,128]{1,2,0:T(8,128)S(1)} custom-call(f32[1,128,128]{2,1,0:T(8,128)S(1)} %get-tuple-element.563), custom_call_target="InvertDiagBlocksLowerTriangular" | custom-call | tf_op jit(solution)/shard_map/cond/branch_1_fun/while/body/eval_jaxpr/jit(cholesky)/cholesky | solution.py:38
  27.1 11.7 %cholesky.273 = f32[128,128]{1,0:T(8,128)S(1)} custom-call(f32[128,128]{1,0:T(8,128)S(1)} %convolution_subtract_fusion.5), custom_call_target="Cholesky" | custom-call | tf_op jit(solution)/shard_map/cond/branch_1_fun/while/body/eval_jaxpr/jit(cholesky)/cholesky | solution.py:38
  38.8 0.7 compare_reduce_fusion
  40.9 4.5 while.74
  41.4 0.6 fusion.397
  42.1 1.3 bitcast_dynamic-update-slice_fusion.14
  43.4 0.6 fusion.397
  44.1 1.3 bitcast_dynamic-update-slice_fusion.14
  45.4 19.7 %custom-call.28 = f32[2,128,128]{1,2,0:T(8,128)S(1)} custom-call(f32[2,128,128]{2,1,0:T(8,128)S(1)} %get-tuple-element.461), custom_call_target="InvertDiagBlocksLowerTriangular" | custom-call | tf_op jit(solution)/shard_map/cond/branch_1_fun/while/body/eval_jaxpr/triangular_solve/custom-call.4 | solution.py:40
  65.2 0.3 fusion.11
  66.3 0.3 fusion.38
  71.0 0.9 copy-done.2
  72.1 88.5 %while.76 = (s32[]{:T(128)}, f32[2,128,128]{2,1,0:T(8,128)S(1)}, f32[1,2,128,128]{3,2,1,0:T(8,128)S(1)}, f32[2,128,128]{1,2,0:T(8,128)S(1)}, s32[]{:T(128)}, /*i...) while((s32[]{:T(128)}, f32[2,128,128]{2,1,0:T(8,128)S(1)}, ...), condition=%wide.region_9.13_spmd, body=%wide.region_6.12_spmd.sunk | while | flops 1133986048 | bytes 15272410 | solution.py:103
  72.2 1.3 collective-permute-start.1
  73.5 3.7 collective-permute-done.1
  77.1 73.4 %collective-permute-start.1 = (f32[2,128,128]{2,1,0:T(8,128)S(1)}, f32[2,128,128]{2,1,0:T(8,128)S(1)}, u32[]{:S(2)}, u32[]{:S(2)}) collective-permute-start(f32[2,128,128]{2,1,0:T(8,128)S(1)} %get-tuple-element.940), channel_id=1, source_target_pairs={{0,8},{8,16},{16,24},{1,9},{9,17},{17,25},{2,10},{10,18},{18,26},{... | collective-permute-start | bytes 393224 | tf_op jit(solution)/shard_map/while/body/eval_jaxpr/ppermute | solution.py:10
  150.6 2.8 collective-permute-done.1
  153.4 4.4 collective-permute-start.1
  157.8 2.5 collective-permute-done.1
  160.9 427.7 %while.77 = (s32[]{:T(128)}, f32[2,128,128]{1,2,0:T(8,128)S(1)}, f32[2,128,128]{2,1,0:T(8,128)S(1)}, s32[]{:T(128)}, f32[1,2,128,128]{3,2,1,0:T(8,128)S(1)}, /*i...) while((s32[]{:T(128)}, f32[2,128,128]{1,2,0:T(8,128)S(1)}, f32[2,128,128]{2,1,0:T(8,128)S(1)}, ...), condition=%wide.region_15.19_spmd, body=%wide.region_12.18_spmd.sunk | while | flops 1133920512 | bytes 14485918 | solution.py:130
  172.9 1.3 collective-permute-start
  174.2 72.9 %collective-permute-done = f32[2,128,128]{2,1,0:T(8,128)S(1)} collective-permute-done((f32[2,128,128]{2,1,0:T(8,128)S(1)}, f32[2,128,128]{2,1,0:T(8,128)S(1)}, u32[]{:S(2)}, u32[]{:S(2)}) %collective-permute-start) | collective-permute-done | bytes 131104 | tf_op jit(solution)/shard_map/while/body/eval_jaxpr/ppermute | solution.py:10
  247.1 1.3 collective-permute-start
  248.5 6.0 collective-permute-done
  254.5 1.3 collective-permute-start
  255.9 264.4 %collective-permute-done = f32[2,128,128]{2,1,0:T(8,128)S(1)} collective-permute-done((f32[2,128,128]{2,1,0:T(8,128)S(1)}, f32[2,128,128]{2,1,0:T(8,128)S(1)}, u32[]{:S(2)}, u32[]{:S(2)}) %collective-permute-start) | collective-permute-done | bytes 131104 | tf_op jit(solution)/shard_map/while/body/eval_jaxpr/ppermute | solution.py:10
  520.3 68.1 %conditional.9 = ((f32[2,128,128]{1,2,0:T(8,128)S(1)}, f32[2,128,128]{2,1,0:T(8,128)S(1)})) conditional(s32[]{:T(128)} %convert_element_type.41, (f32[2,128,128]{1,2,0:T(8,128)S(1)}, f32[2,128,128]{2,1,0:T(8,128)S(1)}) %tuple.213, (f32[1,2,128,128]{3,2,1,0:T(8,128)S(1)}, f32[2,128,128]{2,1,0:T(8,128)S(1)}, f32[1,2,128,128]{3,2,1,0:T(8,128)S(1)}) %tuple.214), branch_computations={%region_13.16_spmd, %region_14.17_spmd} | conditional | flops 1133920512 | bytes 13699295 | solution.py:126
  520.3 0.6 fusion.186
  521.1 11.7 %cholesky.358 = f32[128,128]{1,0:T(8,128)S(1)} custom-call(f32[128,128]{1,0:T(8,128)S(1)} %cholesky.431), custom_call_target="Cholesky" | custom-call | tf_op jit(solution)/shard_map/while/body/eval_jaxpr/cond/branch_1_fun/while/body/eval_jaxpr/jit(cholesky)/cholesky | solution.py:38
  532.9 9.8 %custom-call.35 = f32[1,128,128]{1,2,0:T(8,128)S(1)} custom-call(f32[1,128,128]{2,1,0:T(8,128)S(1)} %get-tuple-element.599), custom_call_target="InvertDiagBlocksLowerTriangular" | custom-call | tf_op jit(solution)/shard_map/while/body/eval_jaxpr/cond/branch_1_fun/while/body/eval_jaxpr/jit(cholesky)/cholesky | solution.py:38
  543.2 11.7 %cholesky.375 = f32[128,128]{1,0:T(8,128)S(1)} custom-call(f32[128,128]{1,0:T(8,128)S(1)} %convolution_subtract_fusion.31), custom_call_target="Cholesky" | custom-call | tf_op jit(solution)/shard_map/while/body/eval_jaxpr/cond/branch_1_fun/while/body/eval_jaxpr/jit(cholesky)/cholesky | solution.py:38
  554.9 0.7 compare_reduce_fusion.6
  557.0 4.0 while.73
  557.0 0.6 fusion.394
  557.7 1.3 bitcast_dynamic-update-slice_fusion.11
  559.0 0.6 fusion.394
  559.7 1.3 bitcast_dynamic-update-slice_fusion.11
  561.0 19.7 %custom-call.37 = f32[2,128,128]{1,2,0:T(8,128)S(1)} custom-call(f32[2,128,128]{2,1,0:T(8,128)S(1)} %get-tuple-element.467), custom_call_target="InvertDiagBlocksLowerTriangular" | custom-call | tf_op jit(solution)/shard_map/while/body/eval_jaxpr/cond/branch_1_fun/while/body/eval_jaxpr/triangular_solve/custom-call.4 | solution.py:40
  580.7 0.3 fusion.187
  581.1 0.4 convolution_subtract_fusion.24
  581.5 0.3 fusion.205
  582.0 0.3 fusion.212
  588.6 0.6 fusion.240
  589.4 11.7 %cholesky.392 = f32[128,128]{1,0:T(8,128)S(1)} custom-call(f32[128,128]{1,0:T(8,128)S(1)} %cholesky.434), custom_call_target="Cholesky" | custom-call | tf_op jit(solution)/shard_map/jit(cholesky)/cholesky | solution.py:38
  601.2 9.8 %custom-call.38 = f32[1,128,128]{1,2,0:T(8,128)S(1)} custom-call(f32[1,128,128]{2,1,0:T(8,128)S(1)} %get-tuple-element.613), custom_call_target="InvertDiagBlocksLowerTriangular" | custom-call | tf_op jit(solution)/shard_map/jit(cholesky)/cholesky | solution.py:38
  611.5 11.7 %cholesky.409 = f32[128,128]{1,0:T(8,128)S(1)} custom-call(f32[128,128]{1,0:T(8,128)S(1)} %convolution_subtract_fusion.37), custom_call_target="Cholesky" | custom-call | tf_op jit(solution)/shard_map/jit(cholesky)/cholesky | solution.py:38
  623.2 0.6 compare_reduce_fusion.8
  625.2 3.8 while.78
  625.2 0.6 fusion.393
  625.8 1.3 bitcast_dynamic-update-slice_fusion.10
  627.1 0.6 fusion.393
  627.7 1.3 bitcast_dynamic-update-slice_fusion.10
  629.0 19.9 %custom-call.40 = f32[2,128,128]{1,2,0:T(8,128)S(1)} custom-call(f32[2,128,128]{2,1,0:T(8,128)S(1)} %get-tuple-element.469), custom_call_target="InvertDiagBlocksLowerTriangular" | custom-call | tf_op jit(solution)/shard_map/triangular_solve/custom-call.4 | solution.py:40
  649.0 0.3 fusion.241
  649.3 0.4 convolution_subtract_fusion.32
  649.7 0.3 fusion.248
  650.3 0.3 fusion.255
  654.3 0.7 maximum_bitcast_fusion
  (159 shorter events, 19.9 us)
Async XLA Ops:
  1.6 0.9 copy-start
  4.3 65.4 %copy-start.1 = (f32[2,128,128]{1,2,0:T(8,128)}, f32[2,128,128]{1,2,0:T(8,128)S(1)}, u32[]{:S(2)}) copy-start(f32[2,128,128]{1,2,0:T(8,128)S(1)} %maximum_subtract_fusion) | copy-start | bytes 393220 | tf_op jit(solution)/shard_map/cond
  71.0 0.9 copy-start.2
  72.2 5.0 collective-permute-start.1
  77.1 76.2 %collective-permute-start.1 = (f32[2,128,128]{2,1,0:T(8,128)S(1)}, f32[2,128,128]{2,1,0:T(8,128)S(1)}, u32[]{:S(2)}, u32[]{:S(2)}) collective-permute-start(f32[2,128,128]{2,1,0:T(8,128)S(1)} %get-tuple-element.940), channel_id=1, source_target_pairs={{0,8},{8,16},{16,24},{1,9},{9,17},{17,25},{2,10},{10,18},{18,26},{... | collective-permute-start | bytes 393224 | tf_op jit(solution)/shard_map/while/body/eval_jaxpr/ppermute | solution.py:10
  153.4 6.9 %collective-permute-start.1 = (f32[2,128,128]{2,1,0:T(8,128)S(1)}, f32[2,128,128]{2,1,0:T(8,128)S(1)}, u32[]{:S(2)}, u32[]{:S(2)}) collective-permute-start(f32[2,128,128]{2,1,0:T(8,128)S(1)} %get-tuple-element.940), channel_id=1, source_target_pairs={{0,8},{8,16},{16,24},{1,9},{9,17},{17,25},{2,10},{10,18},{18,26},{... | collective-permute-start | bytes 393224 | tf_op jit(solution)/shard_map/while/body/eval_jaxpr/ppermute | solution.py:10
  172.9 74.2 %collective-permute-start = (f32[2,128,128]{2,1,0:T(8,128)S(1)}, f32[2,128,128]{2,1,0:T(8,128)S(1)}, u32[]{:S(2)}, u32[]{:S(2)}) collective-permute-start(f32[2,128,128]{2,1,0:T(8,128)S(1)} %copy.19), channel_id=1, source_target_pairs={{8,0},{16,8},{24,16},{9,1},{17,9},{25,17},{10,2},{18,10},{26,18},{... | collective-permute-start | bytes 393224 | tf_op jit(solution)/shard_map/while/body/eval_jaxpr/ppermute | solution.py:10
  247.1 7.3 %collective-permute-start = (f32[2,128,128]{2,1,0:T(8,128)S(1)}, f32[2,128,128]{2,1,0:T(8,128)S(1)}, u32[]{:S(2)}, u32[]{:S(2)}) collective-permute-start(f32[2,128,128]{2,1,0:T(8,128)S(1)} %copy.19), channel_id=1, source_target_pairs={{8,0},{16,8},{24,16},{9,1},{17,9},{25,17},{10,2},{18,10},{26,18},{... | collective-permute-start | bytes 393224 | tf_op jit(solution)/shard_map/while/body/eval_jaxpr/ppermute | solution.py:10
  254.5 265.7 %collective-permute-start = (f32[2,128,128]{2,1,0:T(8,128)S(1)}, f32[2,128,128]{2,1,0:T(8,128)S(1)}, u32[]{:S(2)}, u32[]{:S(2)}) collective-permute-start(f32[2,128,128]{2,1,0:T(8,128)S(1)} %copy.19), channel_id=1, source_target_pairs={{8,0},{16,8},{24,16},{9,1},{17,9},{25,17},{10,2},{18,10},{26,18},{... | collective-permute-start | bytes 393224 | tf_op jit(solution)/shard_map/while/body/eval_jaxpr/ppermute | solution.py:10
where the time goes:
time: 664 us; the launch traced here: 655 us
  waiting for transfers between devices  352 us (53%)
  other arithmetic  163 us (25%)
  starting transfers between devices  83 us (12%)
  matrix products  22.4 us (3%)
  loops' own time  16.7 us (3%)
  local copies, waits for them, and re-layouts  15.5 us (2%)
    ppermute x6, waiting for transfers between devices, from_behind(): lax.ppermute(value, axis, [(source, source + steps) for source in range(f...  352 us
    another operation x18, other arithmetic, invert(): factor = jnp.linalg.cholesky(normal)  102 us
    ppermute x6, starting transfers between devices, from_behind(): lax.ppermute(value, axis, [(source, source + steps) for source in range(f...  83 us
    another operation x11, other arithmetic, invert(): lax.linalg.triangular_solve(factor, middle, left_side=True, lower=True, t...  59.4 us
    dot_general x65, matrix products, matmul_exact(): return jnp.matmul(former, latter, precision=lax.Precision.HIGHEST)  15.8 us
  transfers between devices with their start and end apart: 6, of which 6 were waited for; matrix products, arithmetic and copies ran while one was open for 0% of the time, Pallas kernels for 0%

commit v1 on v0

v1 whole, which is shorter than its diff:
```python
import functools

import jax
import jax.numpy as jnp
from jax import lax
from jax.experimental import pallas as pl
from jax.experimental.pallas import tpu as pltpu
from jax.sharding import PartitionSpec as P

TILE = 8


def dot_full(former, latter):
    return jnp.dot(former, latter, precision=lax.Precision.HIGHEST, preferred_element_type=jnp.float32)


def halves(value):
    high = value.astype(jnp.bfloat16)
    return high, (value - high.astype(jnp.float32)).astype(jnp.bfloat16)


def dot_halves(former, latter):
    former_high, former_low = halves(former)
    latter_high, latter_low = halves(latter)
    dot = functools.partial(jnp.dot, preferred_element_type=jnp.float32)
    return dot(former_high, latter_high) + (dot(former_high, latter_low) + dot(former_low, latter_high))


def complex_product(former, latter, dot=dot_full):
    columns = latter[0].shape[1]
    wide = jnp.concatenate(former, axis=1)
    top = jnp.concatenate(latter, axis=1)
    bottom = jnp.concatenate([-latter[1], latter[0]], axis=1)
    both = dot(wide, jnp.concatenate([top, bottom], axis=0))
    return both[:, :columns], both[:, columns:]


def adjoint(value):
    return value[0].T, -value[1].T


def minus(former, latter):
    return former[0] - latter[0], former[1] - latter[1]


def plus(former, latter):
    return former[0] + latter[0], former[1] + latter[1]


def load(ref):
    return ref[0], ref[1]


def store(ref, value):
    ref[0] = value[0]
    ref[1] = value[1]


def times(ar, ai, br, bi):
    return ar * br - ai * bi, ar * bi + ai * br


def gauss_jordan(re, im):
    size = re.shape[0]
    lane = lax.broadcasted_iota(jnp.int32, (TILE, size), 1)
    sub = lax.broadcasted_iota(jnp.int32, (TILE, size), 0)
    lane_all = lax.broadcasted_iota(jnp.int32, (size, size), 1)

    def column(value, index):
        return jnp.broadcast_to(value[:, index : index + 1], (TILE, size))

    def row(value, index):
        return jnp.broadcast_to(value[index : index + 1, :], (TILE, size))

    past = None
    for start in range(0, size, TILE):
        stop = start + TILE
        pr, pi = re[start:stop, :], im[start:stop, :]
        if past is not None:
            first = start - TILE
            own = (lane >= first) & (lane < start)
            terms = [
                times(column(pr, first + k), column(pi, first + k), row(past[0], k), row(past[1], k))
                for k in range(TILE)
            ]
            while len(terms) > 1:
                terms = [plus(a, b) for a, b in zip(terms[::2], terms[1::2])]
            pr, pi = minus((jnp.where(own, 0.0, pr), jnp.where(own, 0.0, pi)), terms[0])
        spread = [
            (
                jnp.where(sub > TILE, 0.0, column(pr, start + j)),
                jnp.where(sub > TILE, 0.0, column(pi, start + j)),
            )
            for j in range(TILE)
        ]
        for j in range(TILE):
            br, bi = spread[j]
            xr, xi = row(br, j), row(bi, j)
            scale = 1.0 / (xr * xr + xi * xi)
            qr, qi = xr * scale, -(xi * scale)
            at_row = sub == j
            ur, ui = times(br, bi, qr, qi)
            wr, wi = jnp.where(at_row, qr, -ur), jnp.where(at_row, qi, -ui)
            for k in range(j + 1, TILE):
                yr, yi = spread[k]
                tr, ti = times(wr, wi, row(yr, j), row(yi, j))
                spread[k] = (jnp.where(at_row, 0.0, yr) + tr, jnp.where(at_row, 0.0, yi) + ti)
            at_lane = lane == start + j
            tr = jnp.where(at_lane, 1.0, row(pr, j))
            ti = jnp.where(at_lane, 0.0, row(pi, j))
            tr, ti = times(wr, wi, tr, ti)
            clear = at_row | at_lane
            pr = jnp.where(clear, 0.0, pr) + tr
            pi = jnp.where(clear, 0.0, pi) + ti
        ar, ai = re[...], im[...]

        def padded(value, start=start, stop=stop):
            blocks = [value]
            if start:
                blocks.insert(0, jnp.zeros((start, size), jnp.float32))
            if stop < size:
                blocks.append(jnp.zeros((size - stop, size), jnp.float32))
            return jnp.concatenate(blocks, axis=0)

        ur, ui = complex_product((ar, ai), (padded(pr), padded(pi)), dot_halves)
        own = (lane_all >= start) & (lane_all < stop)
        nr = jnp.where(own, 0.0, ar) - ur
        ni = jnp.where(own, 0.0, ai) - ui
        for low, high in ((0, start), (min(stop + TILE, size), size)):
            if high > low:
                re[low:high, :] = nr[low:high]
                im[low:high, :] = ni[low:high]
        re[start:stop, :] = pr
        im[start:stop, :] = pi
        past = (pr, pi)


def inverse(matrix, re, im, refine=False):
    re[...] = matrix[0]
    im[...] = matrix[1]
    gauss_jordan(re, im)
    result = re[...], im[...]
    if refine:
        size = re.shape[0]
        diagonal = lax.broadcasted_iota(jnp.int32, (size, size), 0) == lax.broadcasted_iota(jnp.int32, (size, size), 1)
        pr, pi = complex_product(matrix, result)
        rest = jnp.where(diagonal, 1.0, 0.0) - pr, -pi
        result = plus(result, complex_product(result, rest, dot_halves))
    return result


def begin_kernel(place, onsite, hopping, coupling, matrix, green, re, im):
    size = re.shape[0]
    diagonal = lax.broadcasted_iota(jnp.int32, (size, size), 0) == lax.broadcasted_iota(jnp.int32, (size, size), 1)
    for part in range(2):
        spread = jnp.broadcast_to(onsite[part], (size, size))
        matrix[part] = jnp.where(diagonal, spread, 0.0) - hopping[part, 0]

    @pl.when(place[0] == 0)
    def _():
        link = coupling[0, 0], coupling[1, 0]
        pr, pi = complex_product(adjoint(link), link)
        matrix[0] = matrix[0] - pi
        matrix[1] = matrix[1] + pr

    store(green, inverse(load(matrix), re, im, refine=True))


def links_kernel(place, coupling, behind, inner, inner_adj, outer, outer_adj):
    own = coupling[0, 0], coupling[1, 0]
    other = behind[0, 0], behind[1, 0]

    @pl.when(place[1] == 1)
    def _():
        store(inner, own)
        store(inner_adj, adjoint(own))
        store(outer, adjoint(other))
        store(outer_adj, other)

    @pl.when(place[1] == 0)
    def _():
        store(outer, own)
        store(outer_adj, adjoint(own))
        store(inner, adjoint(other))
        store(inner_adj, other)


def advance_kernel(matrix, incoming, link, link_adj, reduced, green, re, im):
    sigma = complex_product(load(link_adj), complex_product(load(incoming), load(link)))
    value = minus(load(matrix), sigma)
    store(reduced, value)
    store(green, inverse(value, re, im, refine=True))


def meet_kernel(place, reduced, green, incoming, link, link_adj, full, before, after, re, im):
    @pl.when(place[2] == 1)
    def _():
        sigma = complex_product(load(link_adj), complex_product(load(incoming), load(link)))
        store(full, inverse(minus(load(reduced), sigma), re, im, refine=True))

    @pl.when(place[2] == 0)
    def _():
        store(full, load(green))
        store(before, complex_product(load(green), load(link_adj)))
        store(after, complex_product(load(link), load(green)))


def recede_kernel(place, full, green, incoming, before, after, out):
    @pl.when(place[2] == 1)
    def _():
        for part in range(2):
            out[part, 0] = full[part]

    @pl.when(place[2] == 0)
    def _():
        change = complex_product(complex_product(load(before), load(incoming)), load(after))
        value = plus(load(green), change)
        for part in range(2):
            out[part, 0] = value[part]


def on_device(onsite, hopping, coupling):
    assert onsite.shape[1] == 1
    size = onsite.shape[-1]
    pair = jax.ShapeDtypeStruct((2, size, size), jnp.float32)
    scratch = [pltpu.VMEM((size, size), jnp.float32)] * 2
    smem = pl.BlockSpec(memory_space=pltpu.SMEM)
    vmem = pl.BlockSpec(memory_space=pltpu.VMEM)

    def call(kernel, placed, inputs, outputs, scratches=(), **options):
        return pl.pallas_call(
            kernel,
            out_shape=(pair,) * outputs if outputs else jax.ShapeDtypeStruct((2, 1, size, size), jnp.float32),
            in_specs=([smem] if placed else []) + [vmem] * inputs,
            scratch_shapes=scratches,
        )

    count = lax.axis_size("space")
    position = lax.axis_index("space")
    half = count // 2
    is_left = position < half
    is_middle = (position == half - 1) | (position == half) if half else position == 0
    place = jnp.stack([position, is_left.astype(jnp.int32), is_middle.astype(jnp.int32)]).astype(jnp.int32)

    from_right = lax.ppermute(coupling, "space", [(k + 1, k) for k in range(count - 1)])
    matrix, green = call(begin_kernel, True, 3, 2, scratch)(place, onsite, hopping, coupling)
    from_right, _ = lax.optimization_barrier((from_right, green))
    inner, inner_adj, outer, outer_adj = call(links_kernel, True, 2, 4)(place, coupling, from_right)

    inward = [(k, k + 1) for k in range(half - 1)] + [(k, k - 1) for k in range(half + 1, count)]
    reduced = matrix
    for _ in range(max(half, count - half) - 1):
        incoming = lax.ppermute(green, "space", inward)
        reduced, green = call(advance_kernel, False, 4, 2, scratch)(matrix, incoming, inner, inner_adj)

    meeting = [(half - 1, half), (half, half - 1)] if half else []
    incoming = lax.ppermute(green, "space", meeting)
    full, before, after = call(meet_kernel, True, 5, 3, scratch)(place, reduced, green, incoming, outer, outer_adj)

    outward = [(k, k - 1) for k in range(1, half)] + [(k, k + 1) for k in range(half, count - 1)]
    result = full[:, None]
    for _ in range(max(half, count - half) - 1):
        incoming = lax.ppermute(result[:, 0], "space", outward)
        result = call(recede_kernel, True, 5, 0)(place, full, green, incoming, before, after)
    return result


def solution(mesh):
    return jax.shard_map(
        on_device,
        mesh=mesh,
        in_specs=(
            P("energy", "space", None),
            P("energy", "space", None, None),
            P("energy", "space", None, None),
        ),
        out_specs=P("energy", "space", None, None),
        check_vma=False,
    )
```

time: 664 us -> 51.1 us (0.08); the launches traced: 655 us -> 50.8 us
  waiting for transfers between devices: 352 us -> 17.7 us
  other arithmetic: 163 us -> 0.56 us
  starting transfers between devices: 83 us -> 8.48 us
  matrix products: 22.4 us -> 0 us
  Pallas kernels: 0 us -> 21.4 us
  loops' own time: 16.7 us -> 0 us
  local copies, waits for them, and re-layouts: 15.5 us -> 2.57 us
    ppermute x6 -> x4, waiting for transfers between devices: 352 us -> 17.7 us  [the longest x1 17.2 us: on_device(): incoming = lax.ppermute(result[:, 0], 'space', outward)]
    another operation x33 -> x1, other arithmetic: 162 us -> 0.56 us  [on_device(): jnp.stack([position, is_left.astype(jnp.int32), is_middle.astype(jnp.int3...]
    ppermute x6 -> x4, starting transfers between devices: 83 us -> 8.48 us  [the longest x1 5.26 us: on_device(): incoming = lax.ppermute(green, 'space', inward)]
    pallas_call x0 -> x5, Pallas kernels: none -> 21.4 us  [the longest x1 7.47 us: on_device(): call(advance_kernel, False, 4, 2, scratch)]
    another operation x13 -> x0, loops' own time: 16.7 us -> none  [the longest x1 12.2 us: on_device(): backward_final = lax.fori_loop(1, devices, backward_turn, backward_start)]
    dot_general x65 -> x0, matrix products: 15.8 us -> none  [matmul_exact(): return jnp.matmul(former, latter, precision=lax.Precision.HIGHEST)]
    another operation x33 -> x0, local copies, waits for them, and re-layouts: 12.5 us -> none  [the longest x21 11.9 us: invert(): lax.linalg.triangular_solve(factor, middle, left_side=True, lower=True, t...]
    another operation x24 -> x0, matrix products: 6.65 us -> none  [the longest x9 2.9 us: invert(): lax.linalg.triangular_solve(factor, embedded.T, left_side=True, lower=True)]
  transfers between devices with their start and end apart: 6 -> 4, of which waited for: 6 -> 2; matrix products, arithmetic and copies ran while one was open for 0% -> 1% of each run, Pallas kernels for 0% -> 18%
where the time goes in v1:
time: 51.1 us; the launch traced here: 50.8 us
  Pallas kernels  21.4 us (42%)
  waiting for transfers between devices  17.7 us (35%)
  starting transfers between devices  8.48 us (17%)
  local copies, waits for them, and re-layouts  2.57 us (5%)
  other arithmetic  0.56 us (1%)
    ppermute x1, waiting for transfers between devices, on_device(): incoming = lax.ppermute(result[:, 0], 'space', outward)  17.2 us
    pallas_call x1, Pallas kernels, on_device(): call(advance_kernel, False, 4, 2, scratch)  7.47 us
    pallas_call x1, Pallas kernels, on_device(): call(begin_kernel, True, 3, 2, scratch)(place, onsite, hopping, coupling)  7.06 us
    ppermute x1, starting transfers between devices, on_device(): incoming = lax.ppermute(green, 'space', inward)  5.26 us
    unnamed x8, local copies, waits for them, and re-layouts  2.57 us
    pallas_call x1, Pallas kernels, on_device(): call(meet_kernel, True, 5, 3, scratch)  2.53 us
    pallas_call x1, Pallas kernels, on_device(): call(recede_kernel, True, 5, 0)(place, full, green, incoming, before, after)  2.48 us
    pallas_call x1, Pallas kernels, on_device(): call(links_kernel, True, 2, 4)(place, coupling, from_right)  1.9 us
  transfers between devices with their start and end apart: 4, of which 2 were waited for; matrix products, arithmetic and copies ran while one was open for 1% of the time, Pallas kernels for 18%

profile of v1, /device:TPU:0, one launch (start us, length us, event | category | flops | bytes accessed | tf_op | source)
XLA Modules:
  0.0 50.8 jit_solution(6073593092201755190)
XLA Ops:
  0.0 1.3 %collective-permute-start.1 = (f32[2,1,128,128]{3,2,1,0:T(8,128)}, f32[2,1,128,128]{3,2,1,0:T(8,128)S(1)}, u32[]{:S(2)}, u32[]{:S(2)}) collective-permute-start(f32[2,1,128,128]{3,2,1,0:T(8,128)} %coupling.3), channel_id=1, source_target_pairs={{8,0},{16,8},{24,16},{9,1},{17,9},{25,17},{10,2},{18,10},{26,18},{... | collective-permute-start | bytes 393224 | tf_op jit(solution)/shard_map/ppermute | solution.py:245
  1.3 0.6 %pad_add_fusion.place = s32[3]{0:T(128)} fusion(s32[1]{0:T(128)} %bitcast.2, s32[1]{0:T(128)} %bitcast.1, s32[1]{0:T(128)} %bitcast), kind=kLoop, calls=%fused_computation | loop fusion | flops 6 | bytes 24 | tf_op jit(solution)/shard_map/stack | solution.py:243
  1.9 7.1 %shard_map.37 = (f32[2,128,128]{2,1,0:T(8,128)}, f32[2,128,128]{2,1,0:T(8,128)}) custom-call(s32[3]{0:T(128)} %pad_add_fusion.place, f32[2,1,128]{2,1,0:T(1,128)} %onsite.1, f32[2,1,128,128]{3,2,1,0:T(8,128)} %hopping.1, f32[2,1,128,128]{3,2,1,0:T(8,128)} %coupling.3), custom_call_target="tpu_custom_call" | custom-call | tf_op jit(solution)/shard_map/pallas_call | solution.py:246
  8.9 5.3 %collective-permute-start = (f32[2,128,128]{2,1,0:T(8,128)}, f32[2,128,128]{2,1,0:T(8,128)S(1)}, u32[]{:S(2)}, u32[]{:S(2)}) collective-permute-start(f32[2,128,128]{2,1,0:T(8,128)} %get-tuple-element.18), channel_id=1, source_target_pairs={{0,8},{24,16},{1,9},{25,17},{2,10},{26,18},{3,11},{27,19},{4,12},{... | collective-permute-start | bytes 393224 | tf_op jit(solution)/shard_map/ppermute | solution.py:253
  14.2 0.0 collective-permute-done.1.behind
  14.2 0.0 copy-start
  14.2 0.6 %copy-done = f32[2,1,128,128]{3,2,1,0:T(8,128)} copy-done((f32[2,1,128,128]{3,2,1,0:T(8,128)}, f32[2,1,128,128]{3,2,1,0:T(8,128)S(1)}, u32[]{:S(2)}) %copy-start) | copy-done | bytes 131096
  14.8 1.9 %shard_map.38 = (f32[2,128,128]{2,1,0:T(8,128)}, f32[2,128,128]{2,1,0:T(8,128)}, f32[2,128,128]{2,1,0:T(8,128)}, f32[2,128,128]{2,1,0:T(8,128)}) custom-call(s32[3]{0:T(128)} %pad_add_fusion.place, f32[2,1,128,128]{3,2,1,0:T(8,128)} %coupling.3, f32[2,1,128,128]{3,2,1,0:T(8,128)} %copy-done), custom_call_target="tpu_custom_call" | custom-call | tf_op jit(solution)/shard_map/pallas_call | solution.py:248
  16.7 0.5 collective-permute-done.incoming
  17.2 0.0 copy-start.1
  17.2 0.7 %copy-done.1 = f32[2,128,128]{2,1,0:T(8,128)} copy-done((f32[2,128,128]{2,1,0:T(8,128)}, f32[2,128,128]{2,1,0:T(8,128)S(1)}, u32[]{:S(2)}) %copy-start.1) | copy-done | bytes 131096
  17.9 7.5 %shard_map.39 = (f32[2,128,128]{2,1,0:T(8,128)}, f32[2,128,128]{2,1,0:T(8,128)}) custom-call(f32[2,128,128]{2,1,0:T(8,128)} %get-tuple-element.17.matrix, f32[2,128,128]{2,1,0:T(8,128)} %copy-done.1, f32[2,128,128]{2,1,0:T(8,128)} %get-tuple-element.20.link, f32[2,128,128]{2,1,0:T(8,128)} %get-tuple-element.21.link_adj), custom_call_target="tpu_custom_call" | custom-call | tf_op jit(solution)/shard_map/pallas_call | solution.py:254
  25.4 0.7 %collective-permute-start.2 = (f32[2,128,128]{2,1,0:T(8,128)}, f32[2,128,128]{2,1,0:T(8,128)S(1)}, u32[]{:S(2)}, u32[]{:S(2)}) collective-permute-start(f32[2,128,128]{2,1,0:T(8,128)} %get-tuple-element.23.green), channel_id=1, source_target_pairs={{8,16},{16,8},{9,17},{17,9},{10,18},{18,10},{11,19},{19,11},{12,20... | collective-permute-start | bytes 393224 | tf_op jit(solution)/shard_map/ppermute | solution.py:257
  26.0 0.0 collective-permute-done.2.incoming
  26.0 0.0 copy-start.2
  26.1 0.6 %copy-done.2 = f32[2,128,128]{2,1,0:T(8,128)} copy-done((f32[2,128,128]{2,1,0:T(8,128)}, f32[2,128,128]{2,1,0:T(8,128)S(1)}, u32[]{:S(2)}) %copy-start.2) | copy-done | bytes 131096
  26.7 2.5 %shard_map.40 = (f32[2,128,128]{2,1,0:T(8,128)}, f32[2,128,128]{2,1,0:T(8,128)}, f32[2,128,128]{2,1,0:T(8,128)}) custom-call(s32[3]{0:T(128)} %pad_add_fusion.place, f32[2,128,128]{2,1,0:T(8,128)} %get-tuple-element.22.reduced, f32[2,128,128]{2,1,0:T(8,128)} %get-tuple-element.23.green, f32[2,128,128]{2,1,0:T(8,128)} %copy-done.2, ...), custom_call_target="tpu_custom_call" | custom-call | tf_op jit(solution)/shard_map/pallas_call | solution.py:258
  29.2 1.3 %collective-permute-start.3 = (f32[2,128,128]{2,1,0:T(8,128)}, f32[2,128,128]{2,1,0:T(8,128)S(1)}, u32[]{:S(2)}, u32[]{:S(2)}) collective-permute-start(f32[2,128,128]{2,1,0:T(8,128)} %get-tuple-element.26.full), channel_id=1, source_target_pairs={{8,0},{16,24},{9,1},{17,25},{10,2},{18,26},{11,3},{19,27},{12,4},{... | collective-permute-start | bytes 393224 | tf_op jit(solution)/shard_map/ppermute | solution.py:263
  30.5 17.2 %collective-permute-done.3.incoming = f32[2,128,128]{2,1,0:T(8,128)S(1)} collective-permute-done((f32[2,128,128]{2,1,0:T(8,128)}, f32[2,128,128]{2,1,0:T(8,128)S(1)}, u32[]{:S(2)}, u32[]{:S(2)}) %collective-permute-start.3) | collective-permute-done | bytes 131104 | tf_op jit(solution)/shard_map/ppermute | solution.py:263
  47.7 0.0 copy-start.3
  47.7 0.6 %copy-done.3 = f32[2,128,128]{2,1,0:T(8,128)} copy-done((f32[2,128,128]{2,1,0:T(8,128)}, f32[2,128,128]{2,1,0:T(8,128)S(1)}, u32[]{:S(2)}) %copy-start.3) | copy-done | bytes 131096
  48.3 2.5 %shard_map.41 = f32[2,1,128,128]{3,2,1,0:T(8,128)} custom-call(s32[3]{0:T(128)} %pad_add_fusion.place, f32[2,128,128]{2,1,0:T(8,128)} %get-tuple-element.26.full, f32[2,128,128]{2,1,0:T(8,128)} %get-tuple-element.23.green, f32[2,128,128]{2,1,0:T(8,128)} %copy-done.3, f32[2,128,128]{2,1,0:T(8,128)} %get-tuple-element.27.before, ...), custom_call_target="tpu_custom_call" | custom-call | tf_op jit(solution)/shard_map/pallas_call | solution.py:264
Async XLA Ops:
  0.0 14.2 %collective-permute-start.1 = (f32[2,1,128,128]{3,2,1,0:T(8,128)}, f32[2,1,128,128]{3,2,1,0:T(8,128)S(1)}, u32[]{:S(2)}, u32[]{:S(2)}) collective-permute-start(f32[2,1,128,128]{3,2,1,0:T(8,128)} %coupling.3), channel_id=1, source_target_pairs={{8,0},{16,8},{24,16},{9,1},{17,9},{25,17},{10,2},{18,10},{26,18},{... | collective-permute-start | bytes 393224 | tf_op jit(solution)/shard_map/ppermute | solution.py:245
  8.9 8.3 %collective-permute-start = (f32[2,128,128]{2,1,0:T(8,128)}, f32[2,128,128]{2,1,0:T(8,128)S(1)}, u32[]{:S(2)}, u32[]{:S(2)}) collective-permute-start(f32[2,128,128]{2,1,0:T(8,128)} %get-tuple-element.18), channel_id=1, source_target_pairs={{0,8},{24,16},{1,9},{25,17},{2,10},{26,18},{3,11},{27,19},{4,12},{... | collective-permute-start | bytes 393224 | tf_op jit(solution)/shard_map/ppermute | solution.py:253
  14.2 0.6 %copy-start = (f32[2,1,128,128]{3,2,1,0:T(8,128)}, f32[2,1,128,128]{3,2,1,0:T(8,128)S(1)}, u32[]{:S(2)}) copy-start(f32[2,1,128,128]{3,2,1,0:T(8,128)S(1)} %collective-permute-done.1.behind) | copy-start | bytes 393220
  17.2 0.7 %copy-start.1 = (f32[2,128,128]{2,1,0:T(8,128)}, f32[2,128,128]{2,1,0:T(8,128)S(1)}, u32[]{:S(2)}) copy-start(f32[2,128,128]{2,1,0:T(8,128)S(1)} %collective-permute-done.incoming) | copy-start | bytes 393220
  25.4 0.7 %collective-permute-start.2 = (f32[2,128,128]{2,1,0:T(8,128)}, f32[2,128,128]{2,1,0:T(8,128)S(1)}, u32[]{:S(2)}, u32[]{:S(2)}) collective-permute-start(f32[2,128,128]{2,1,0:T(8,128)} %get-tuple-element.23.green), channel_id=1, source_target_pairs={{8,16},{16,8},{9,17},{17,9},{10,18},{18,10},{11,19},{19,11},{12,20... | collective-permute-start | bytes 393224 | tf_op jit(solution)/shard_map/ppermute | solution.py:257
  26.0 0.7 %copy-start.2 = (f32[2,128,128]{2,1,0:T(8,128)}, f32[2,128,128]{2,1,0:T(8,128)S(1)}, u32[]{:S(2)}) copy-start(f32[2,128,128]{2,1,0:T(8,128)S(1)} %collective-permute-done.2.incoming) | copy-start | bytes 393220
  29.2 18.5 %collective-permute-start.3 = (f32[2,128,128]{2,1,0:T(8,128)}, f32[2,128,128]{2,1,0:T(8,128)S(1)}, u32[]{:S(2)}, u32[]{:S(2)}) collective-permute-start(f32[2,128,128]{2,1,0:T(8,128)} %get-tuple-element.26.full), channel_id=1, source_target_pairs={{8,0},{16,24},{9,1},{17,25},{10,2},{18,26},{11,3},{19,27},{12,4},{... | collective-permute-start | bytes 393224 | tf_op jit(solution)/shard_map/ppermute | solution.py:263
  47.7 0.6 %copy-start.3 = (f32[2,128,128]{2,1,0:T(8,128)}, f32[2,128,128]{2,1,0:T(8,128)S(1)}, u32[]{:S(2)}) copy-start(f32[2,128,128]{2,1,0:T(8,128)S(1)} %collective-permute-done.3.incoming) | copy-start | bytes 393220

commit v2 on v1

--- a/solution.py
+++ b/solution.py
@@ -219,8 +219,7 @@
             out[part, 0] = value[part]
 
 
-def on_device(onsite, hopping, coupling):
-    assert onsite.shape[1] == 1
+def chain_of_slabs(onsite, hopping, coupling):
     size = onsite.shape[-1]
     pair = jax.ShapeDtypeStruct((2, size, size), jnp.float32)
     scratch = [pltpu.VMEM((size, size), jnp.float32)] * 2
@@ -263,6 +262,115 @@
         incoming = lax.ppermute(result[:, 0], "space", outward)
         result = call(recede_kernel, True, 5, 0)(place, full, green, incoming, before, after)
     return result
+
+
+def choose(condition, former, latter):
+    return jnp.where(condition, former[0], latter[0]), jnp.where(condition, former[1], latter[1])
+
+
+def open_kernel(onsite, hopping, coupling, message, re, im):
+    position = lax.axis_index("space")
+    is_outer = (position == 0) | (position == 3)
+    size = re.shape[0]
+    diagonal = lax.broadcasted_iota(jnp.int32, (size, size), 0) == lax.broadcasted_iota(jnp.int32, (size, size), 1)
+    for part in range(2):
+        spread = jnp.broadcast_to(onsite[part], (size, size))
+        message[part] = jnp.where(diagonal, spread, 0.0) - hopping[part, 0]
+        message[2 + part] = coupling[part, 0]
+
+    @pl.when(position == 0)
+    def _():
+        link = message[2], message[3]
+        pr, pi = complex_product(adjoint(link), link)
+        message[0] = message[0] - pi
+        message[1] = message[1] + pr
+
+    @pl.when(is_outer)
+    def _():
+        store(message, inverse(load(message), re, im, refine=True))
+
+
+def half_kernel(mine, theirs, reduced, before, after, message, re, im):
+    position = lax.axis_index("space")
+    is_left = position < 2
+    is_outer = (position == 0) | (position == 3)
+    end = choose(is_outer, (mine[0], mine[1]), (theirs[0], theirs[1]))
+    inner = choose(is_outer, (theirs[0], theirs[1]), (mine[0], mine[1]))
+    use_mine = is_left ^ is_outer
+    link = choose(use_mine, (mine[2], mine[3]), (theirs[2], theirs[3]))
+    link_adj = adjoint(link)
+    inward = choose(is_left, link, link_adj)
+    outward = choose(is_left, link_adj, link)
+    ahead = complex_product(end, inward)
+    store(before, ahead)
+    store(after, complex_product(outward, end))
+    value = minus(inner, complex_product(outward, ahead))
+    store(reduced, value)
+    green = inverse(value, re, im, refine=True)
+    store(message, green)
+
+    @pl.when(jnp.logical_not(is_left))
+    def _():
+        middle = choose(is_outer, (theirs[2], theirs[3]), (mine[2], mine[3]))
+        store(message, complex_product(complex_product(middle, load(message)), adjoint(middle)))
+
+
+def close_kernel(mine, theirs, reduced, before, after, incoming, out, full, re, im):
+    position = lax.axis_index("space")
+    is_left = position < 2
+    is_outer = (position == 0) | (position == 3)
+    store(full, load(incoming))
+
+    @pl.when(jnp.logical_not(is_left))
+    def _():
+        middle = choose(is_outer, (theirs[2], theirs[3]), (mine[2], mine[3]))
+        store(full, complex_product(adjoint(middle), complex_product(load(incoming), middle)))
+
+    green = inverse(minus(load(reduced), load(full)), re, im, refine=True)
+
+    @pl.when(jnp.logical_not(is_outer))
+    def _():
+        out[0, 0] = green[0]
+        out[1, 0] = green[1]
+
+    @pl.when(is_outer)
+    def _():
+        store(full, green)
+        change = complex_product(complex_product(load(before), load(full)), load(after))
+        out[0, 0] = mine[0] + change[0]
+        out[1, 0] = mine[1] + change[1]
+
+
+def four_slabs(onsite, hopping, coupling):
+    size = onsite.shape[-1]
+    scratch = [pltpu.VMEM((size, size), jnp.float32)] * 2
+    pair = pltpu.VMEM((2, size, size), jnp.float32)
+    vmem = pl.BlockSpec(memory_space=pltpu.VMEM)
+
+    def on_chip(value):
+        return pltpu.with_memory_space_constraint(value, pltpu.VMEM)
+
+    mine = pl.pallas_call(
+        open_kernel, out_shape=pltpu.VMEM((4, size, size), jnp.float32), in_specs=[vmem] * 3, scratch_shapes=scratch
+    )(onsite, hopping, coupling)
+    theirs = on_chip(lax.ppermute(mine, "space", [(0, 1), (1, 0), (2, 3), (3, 2)]))
+    reduced, before, after, message = pl.pallas_call(
+        half_kernel, out_shape=(pair,) * 4, in_specs=[vmem] * 2, scratch_shapes=scratch
+    )(mine, theirs)
+    incoming = on_chip(lax.ppermute(message, "space", [(0, 3), (3, 0), (1, 2), (2, 1)]))
+    return pl.pallas_call(
+        close_kernel,
+        out_shape=jax.ShapeDtypeStruct(hopping.shape, jnp.float32),
+        in_specs=[vmem] * 6,
+        scratch_shapes=[pltpu.VMEM((2, size, size), jnp.float32)] + scratch,
+    )(mine, theirs, reduced, before, after, incoming)
+
+
+def on_device(onsite, hopping, coupling):
+    assert onsite.shape[1] == 1
+    if lax.axis_size("space") == 4:
+        return four_slabs(onsite, hopping, coupling)
+    return chain_of_slabs(onsite, hopping, coupling)
 
 
 def solution(mesh):

time: 51.1 us -> 39.5 us (0.77)
  waiting for transfers between devices: 17.7 us -> 11.6 us
  starting transfers between devices: 8.48 us -> 4.82 us
  local copies, waits for them, and re-layouts: 2.57 us -> 1.94 us
  other arithmetic: 0.56 us -> 0 us
    ppermute x4 -> x2, waiting for transfers between devices: 17.7 us -> 11.6 us  [the longest x1 8.69 us: four_slabs(): lax.ppermute(mine, 'space', [(0, 1), (1, 0), (2, 3), (3, 2)])]
    ppermute x4 -> x2, starting transfers between devices: 8.48 us -> 4.82 us  [the longest x1 4.74 us: four_slabs(): lax.ppermute(message, 'space', [(0, 3), (3, 0), (1, 2), (2, 1)])]
    unnamed x8, local copies, waits for them, and re-layouts: 2.57 us -> 1.94 us
    pallas_call x5 -> x3, Pallas kernels: 21.4 us -> 20.9 us  [the longest x1 7.66 us: four_slabs(): pl.pallas_call(close_kernel, out_shape=jax.ShapeDtypeStruct(hopping.shape...]
    another operation x1 -> x0, other arithmetic: 0.56 us -> none  [on_device(): jnp.stack([position, is_left.astype(jnp.int32), is_middle.astype(jnp.int3...]
  transfers between devices with their start and end apart: 4 -> 2, of which waited for: 2 -> 2; matrix products, arithmetic and copies ran while one was open for 1% -> 0% of each run, Pallas kernels for 18% -> 0%
where the time goes in v2:
time: 39.5 us; the launch traced here: 39.3 us
  Pallas kernels  20.9 us (53%)
  waiting for transfers between devices  11.6 us (29%)
  starting transfers between devices  4.82 us (12%)
  local copies, waits for them, and re-layouts  1.94 us (5%)
    ppermute x1, waiting for transfers between devices, four_slabs(): lax.ppermute(mine, 'space', [(0, 1), (1, 0), (2, 3), (3, 2)])  8.69 us
    pallas_call x1, Pallas kernels, four_slabs(): pl.pallas_call(close_kernel, out_shape=jax.ShapeDtypeStruct(hopping.shape...  7.66 us
    pallas_call x1, Pallas kernels, four_slabs(): pl.pallas_call(half_kernel, out_shape=(pair,) * 4, in_specs=[vmem] * 2, s...  6.81 us
    pallas_call x1, Pallas kernels, four_slabs(): pl.pallas_call(open_kernel, out_shape=pltpu.VMEM((4, size, size), jnp.flo...  6.41 us
    ppermute x1, starting transfers between devices, four_slabs(): lax.ppermute(message, 'space', [(0, 3), (3, 0), (1, 2), (2, 1)])  4.74 us
    ppermute x1, waiting for transfers between devices, four_slabs(): lax.ppermute(message, 'space', [(0, 3), (3, 0), (1, 2), (2, 1)])  2.95 us
    unnamed x8, local copies, waits for them, and re-layouts  1.94 us
  transfers between devices with their start and end apart: 2, of which 2 were waited for; matrix products, arithmetic and copies ran while one was open for 0% of the time, Pallas kernels for 0%

profile of v2, /device:TPU:0, one launch (start us, length us, event | category | flops | bytes accessed | tf_op | source)
XLA Modules:
  0.0 39.3 jit_solution(4696021868663746669)
XLA Ops:
  0.0 6.4 %shard_map.37.mine = f32[4,128,128]{2,1,0:T(8,128)S(1)} custom-call(f32[2,1,128]{2,1,0:T(1,128)} %onsite.1, f32[2,1,128,128]{3,2,1,0:T(8,128)} %hopping.1, f32[2,1,128,128]{3,2,1,0:T(8,128)} %coupling.1), custom_call_target="tpu_custom_call" | custom-call | tf_op jit(solution)/shard_map/pallas_call | solution.py:353
  6.4 0.0 copy-start
  6.4 0.1 collective-permute-start
  6.5 8.7 %collective-permute-done.theirs = f32[4,128,128]{2,1,0:T(8,128)S(1)} collective-permute-done((f32[4,128,128]{2,1,0:T(8,128)S(1)}, f32[4,128,128]{2,1,0:T(8,128)S(1)}, u32[]{:S(2)}, u32[]{:S(2)}) %collective-permute-start) | collective-permute-done | bytes 262176 | tf_op jit(solution)/shard_map/ppermute | solution.py:356
  15.2 0.0 copy-done
  15.2 6.8 %shard_map.38 = (f32[2,128,128]{2,1,0:T(8,128)S(1)}, f32[2,128,128]{2,1,0:T(8,128)S(1)}, f32[2,128,128]{2,1,0:T(8,128)S(1)}, f32[2,128,128]{2,1,0:T(8,128)S(1)}) custom-call(f32[4,128,128]{2,1,0:T(8,128)} %copy-done, f32[4,128,128]{2,1,0:T(8,128)S(1)} %collective-permute-done.theirs), custom_call_target="tpu_custom_call" | custom-call | tf_op jit(solution)/shard_map/pallas_call | solution.py:357
  22.0 0.0 copy-start.1
  22.0 0.6 %copy-done.1 = f32[2,128,128]{2,1,0:T(8,128)} copy-done((f32[2,128,128]{2,1,0:T(8,128)}, f32[2,128,128]{2,1,0:T(8,128)S(1)}, u32[]{:S(2)}) %copy-start.1) | copy-done | bytes 131096
  22.7 0.0 copy-start.2
  22.7 0.6 %copy-done.2 = f32[2,128,128]{2,1,0:T(8,128)} copy-done((f32[2,128,128]{2,1,0:T(8,128)}, f32[2,128,128]{2,1,0:T(8,128)S(1)}, u32[]{:S(2)}) %copy-start.2) | copy-done | bytes 131096
  23.3 0.0 copy-start.3
  23.3 0.6 %copy-done.3 = f32[2,128,128]{2,1,0:T(8,128)} copy-done((f32[2,128,128]{2,1,0:T(8,128)}, f32[2,128,128]{2,1,0:T(8,128)S(1)}, u32[]{:S(2)}) %copy-start.3) | copy-done | bytes 131096
  24.0 4.7 %collective-permute-start.1 = (f32[2,128,128]{2,1,0:T(8,128)S(1)}, f32[2,128,128]{2,1,0:T(8,128)S(1)}, u32[]{:S(2)}, u32[]{:S(2)}) collective-permute-start(f32[2,128,128]{2,1,0:T(8,128)S(1)} %get-tuple-element.12), channel_id=1, source_target_pairs={{0,24},{24,0},{8,16},{16,8},{1,25},{25,1},{9,17},{17,9},{2,26},{26... | collective-permute-start | bytes 393224 | tf_op jit(solution)/shard_map/ppermute | solution.py:360
  28.7 2.9 %collective-permute-done.1.incoming = f32[2,128,128]{2,1,0:T(8,128)S(1)} collective-permute-done((f32[2,128,128]{2,1,0:T(8,128)S(1)}, f32[2,128,128]{2,1,0:T(8,128)S(1)}, u32[]{:S(2)}, u32[]{:S(2)}) %collective-permute-start.1) | collective-permute-done | bytes 131104 | tf_op jit(solution)/shard_map/ppermute | solution.py:360
  31.7 7.7 %shard_map.39 = f32[2,1,128,128]{3,2,1,0:T(8,128)} custom-call(f32[4,128,128]{2,1,0:T(8,128)} %copy-done, f32[4,128,128]{2,1,0:T(8,128)S(1)} %collective-permute-done.theirs, f32[2,128,128]{2,1,0:T(8,128)} %copy-done.1, f32[2,128,128]{2,1,0:T(8,128)} %copy-done.2, f32[2,128,128]{2,1,0:T(8,128)} %copy-done.3, f32[2,128,128]{2,1,0:T(8,128)S(1)} %collective-permute-done.1.incoming), custom_call_target="tpu_custom_call" | custom-call | tf_op jit(solution)/shard_map/pallas_call | solution.py:361
Async XLA Ops:
  6.4 8.8 %copy-start = (f32[4,128,128]{2,1,0:T(8,128)}, f32[4,128,128]{2,1,0:T(8,128)S(1)}, u32[]{:S(2)}) copy-start(f32[4,128,128]{2,1,0:T(8,128)S(1)} %shard_map.37.mine) | copy-start | bytes 786436
  6.4 8.8 %collective-permute-start = (f32[4,128,128]{2,1,0:T(8,128)S(1)}, f32[4,128,128]{2,1,0:T(8,128)S(1)}, u32[]{:S(2)}, u32[]{:S(2)}) collective-permute-start(f32[4,128,128]{2,1,0:T(8,128)S(1)} %shard_map.37.mine), channel_id=1, source_target_pairs={{0,8},{8,0},{16,24},{24,16},{1,9},{9,1},{17,25},{25,17},{2,10},{10... | collective-permute-start | bytes 786440 | tf_op jit(solution)/shard_map/ppermute | solution.py:356
  22.0 0.7 %copy-start.1 = (f32[2,128,128]{2,1,0:T(8,128)}, f32[2,128,128]{2,1,0:T(8,128)S(1)}, u32[]{:S(2)}) copy-start(f32[2,128,128]{2,1,0:T(8,128)S(1)} %get-tuple-element.9.reduced) | copy-start | bytes 393220
  22.7 0.7 %copy-start.2 = (f32[2,128,128]{2,1,0:T(8,128)}, f32[2,128,128]{2,1,0:T(8,128)S(1)}, u32[]{:S(2)}) copy-start(f32[2,128,128]{2,1,0:T(8,128)S(1)} %get-tuple-element.10.before) | copy-start | bytes 393220
  23.3 0.6 %copy-start.3 = (f32[2,128,128]{2,1,0:T(8,128)}, f32[2,128,128]{2,1,0:T(8,128)S(1)}, u32[]{:S(2)}) copy-start(f32[2,128,128]{2,1,0:T(8,128)S(1)} %get-tuple-element.11.after) | copy-start | bytes 393220
  24.0 7.7 %collective-permute-start.1 = (f32[2,128,128]{2,1,0:T(8,128)S(1)}, f32[2,128,128]{2,1,0:T(8,128)S(1)}, u32[]{:S(2)}, u32[]{:S(2)}) collective-permute-start(f32[2,128,128]{2,1,0:T(8,128)S(1)} %get-tuple-element.12), channel_id=1, source_target_pairs={{0,24},{24,0},{8,16},{16,8},{1,25},{25,1},{9,17},{17,9},{2,26},{26... | collective-permute-start | bytes 393224 | tf_op jit(solution)/shard_map/ppermute | solution.py:360

commit v3 on v1

--- a/solution.py
+++ b/solution.py
@@ -219,8 +219,7 @@
             out[part, 0] = value[part]
 
 
-def on_device(onsite, hopping, coupling):
-    assert onsite.shape[1] == 1
+def chain_of_slabs(onsite, hopping, coupling):
     size = onsite.shape[-1]
     pair = jax.ShapeDtypeStruct((2, size, size), jnp.float32)
     scratch = [pltpu.VMEM((size, size), jnp.float32)] * 2
@@ -263,6 +262,158 @@
         incoming = lax.ppermute(result[:, 0], "space", outward)
         result = call(recede_kernel, True, 5, 0)(place, full, green, incoming, before, after)
     return result
+
+
+def choose(condition, former, latter):
+    return jnp.where(condition, former[0], latter[0]), jnp.where(condition, former[1], latter[1])
+
+
+def whereabouts():
+    position = lax.axis_index("space")
+    return position < 2, (position == 0) | (position == 3)
+
+
+def slab_kernel(onsite, hopping, coupling, mine):
+    size = hopping.shape[-1]
+    diagonal = lax.broadcasted_iota(jnp.int32, (size, size), 0) == lax.broadcasted_iota(jnp.int32, (size, size), 1)
+    for part in range(2):
+        spread = jnp.broadcast_to(onsite[part], (size, size))
+        mine[part] = jnp.where(diagonal, spread, 0.0) - hopping[part, 0]
+        mine[2 + part] = coupling[part, 0]
+
+
+def end_kernel(mine, end, message, re, im):
+    is_left, is_outer = whereabouts()
+
+    @pl.when(is_outer)
+    def _():
+        link = mine[2], mine[3]
+        store(end, (mine[0], mine[1]))
+
+        @pl.when(is_left)
+        def _():
+            pr, pi = complex_product(adjoint(link), link)
+            end[0] = end[0] - pi
+            end[1] = end[1] + pr
+
+        green = inverse(load(end), re, im, refine=True)
+        store(end, green)
+        store(message, green)
+
+        @pl.when(jnp.logical_not(is_left))
+        def _():
+            store(message, complex_product(link, complex_product(load(end), adjoint(link))))
+
+
+def send_half(is_left, middle, green, message):
+    store(message, green)
+
+    @pl.when(jnp.logical_not(is_left))
+    def _():
+        store(message, complex_product(middle, complex_product(load(message), adjoint(middle))))
+
+
+def outer_kernel(mine, theirs, end, reduced, before, after, message, re, im):
+    is_left, is_outer = whereabouts()
+
+    @pl.when(is_outer)
+    def _():
+        link = choose(is_left, (theirs[2], theirs[3]), (mine[2], mine[3]))
+        link_adj = adjoint(link)
+        inward = choose(is_left, link, link_adj)
+        outward = choose(is_left, link_adj, link)
+        ahead = complex_product(load(end), inward)
+        store(before, ahead)
+        store(after, complex_product(outward, load(end)))
+        value = minus((theirs[0], theirs[1]), complex_product(outward, ahead))
+        store(reduced, value)
+        send_half(is_left, (theirs[2], theirs[3]), inverse(value, re, im, refine=True), message)
+
+
+def inner_kernel(mine, incoming, outer_reduced, outer_message, reduced, message, re, im):
+    is_left, is_outer = whereabouts()
+
+    @pl.when(is_outer)
+    def _():
+        store(reduced, load(outer_reduced))
+        store(message, load(outer_message))
+
+    @pl.when(jnp.logical_not(is_outer))
+    def _():
+        link = mine[2], mine[3]
+        store(reduced, load(incoming))
+
+        @pl.when(is_left)
+        def _():
+            store(reduced, complex_product(adjoint(link), complex_product(load(incoming), link)))
+
+        value = minus((mine[0], mine[1]), load(reduced))
+        store(reduced, value)
+        send_half(is_left, link, inverse(value, re, im, refine=True), message)
+
+
+def close_kernel(mine, theirs, end, before, after, reduced, incoming, out, full, re, im):
+    is_left, is_outer = whereabouts()
+    store(full, load(incoming))
+
+    @pl.when(jnp.logical_not(is_left))
+    def _():
+        middle = choose(is_outer, (theirs[2], theirs[3]), (mine[2], mine[3]))
+        store(full, complex_product(adjoint(middle), complex_product(load(incoming), middle)))
+
+    green = inverse(minus(load(reduced), load(full)), re, im, refine=True)
+
+    @pl.when(jnp.logical_not(is_outer))
+    def _():
+        out[0, 0] = green[0]
+        out[1, 0] = green[1]
+
+    @pl.when(is_outer)
+    def _():
+        store(full, green)
+        change = complex_product(complex_product(load(before), load(full)), load(after))
+        out[0, 0] = end[0] + change[0]
+        out[1, 0] = end[1] + change[1]
+
+
+def four_slabs(onsite, hopping, coupling):
+    size = onsite.shape[-1]
+    scratch = [pltpu.VMEM((size, size), jnp.float32)] * 2
+    pair = pltpu.VMEM((2, size, size), jnp.float32)
+    within_halves = [(0, 1), (1, 0), (2, 3), (3, 2)]
+    across = [(0, 3), (3, 0), (1, 2), (2, 1)]
+
+    def call(kernel, out_shape, scratch_shapes, *operands):
+        vmem = pl.BlockSpec(memory_space=pltpu.VMEM)
+        return pl.pallas_call(
+            kernel, out_shape=out_shape, in_specs=[vmem] * len(operands), scratch_shapes=scratch_shapes
+        )(*operands)
+
+    def on_chip(*values):
+        return [pltpu.with_memory_space_constraint(value, pltpu.VMEM) for value in values]
+
+    mine = call(slab_kernel, pltpu.VMEM((4, size, size), jnp.float32), [], onsite, hopping, coupling)
+    theirs = lax.ppermute(mine, "space", within_halves)
+    mine, theirs = on_chip(mine, theirs)
+    end, message = call(end_kernel, (pair,) * 2, scratch, mine)
+    end, message = on_chip(end, message)
+    incoming = on_chip(lax.ppermute(message, "space", within_halves))[0]
+    outer = on_chip(*call(outer_kernel, (pair,) * 4, scratch, mine, theirs, end))
+    inner = on_chip(*call(inner_kernel, (pair,) * 2, scratch, mine, incoming, outer[0], outer[3]))
+    incoming = on_chip(lax.ppermute(inner[1], "space", across))[0]
+    return call(
+        close_kernel,
+        jax.ShapeDtypeStruct(hopping.shape, jnp.float32),
+        [pltpu.VMEM((2, size, size), jnp.float32)] + scratch,
+        *(mine, theirs, end, outer[1], outer[2], inner[0], incoming),
+    )
+
+
+def on_device(onsite, hopping, coupling):
+    assert onsite.shape[1] == 1
+    if lax.axis_size("space") == 4:
+        return four_slabs(onsite, hopping, coupling)
+    return chain_of_slabs(onsite, hopping, coupling)
 
 
 def solution(mesh):

time: 51.1 us -> 31.8 us (0.62)
  the two profiles are of different devices: /device:TPU:0 before, /device:TPU:16 now
where the time goes in v3:
time: 31.8 us; the launch traced here: 31.7 us
  Pallas kernels  13.7 us (43%)
  waiting for transfers between devices  9.77 us (31%)
  starting transfers between devices  8.13 us (26%)
    pallas_call x5, Pallas kernels, call(): pl.pallas_call(kernel, out_shape=out_shape, in_specs=[vmem] * len(operand...  13.7 us
    ppermute x1, waiting for transfers between devices, four_slabs(): incoming = on_chip(lax.ppermute(inner[1], 'space', across))[0]  6.56 us
    ppermute x1, starting transfers between devices, four_slabs(): incoming = on_chip(lax.ppermute(message, 'space', within_halves))[0]  6.41 us
    ppermute x1, waiting for transfers between devices, four_slabs(): incoming = on_chip(lax.ppermute(message, 'space', within_halves))[0]  3.15 us
    ppermute x1, starting transfers between devices, four_slabs(): theirs = lax.ppermute(mine, 'space', within_halves)  1.64 us
  transfers between devices with their start and end apart: 3, of which 3 were waited for; matrix products, arithmetic and copies ran while one was open for 0% of the time, Pallas kernels for 0%

profile of v3, /device:TPU:16, one launch (start us, length us, event | category | flops | bytes accessed | tf_op | source)
XLA Modules:
  0.0 31.7 jit_solution(455132414865659259)
XLA Ops:
  0.0 1.0 %shard_map.37.mine = f32[4,128,128]{2,1,0:T(8,128)S(1)} custom-call(f32[2,1,128]{2,1,0:T(1,128)} %onsite.1, f32[2,1,128,128]{3,2,1,0:T(8,128)} %hopping.1, f32[2,1,128,128]{3,2,1,0:T(8,128)} %coupling.1), custom_call_target="tpu_custom_call" | custom-call | tf_op jit(solution)/shard_map/pallas_call | solution.py:388
  1.0 1.6 %collective-permute-start = (f32[4,128,128]{2,1,0:T(8,128)S(1)}, f32[4,128,128]{2,1,0:T(8,128)S(1)}, u32[]{:S(2)}, u32[]{:S(2)}) collective-permute-start(f32[4,128,128]{2,1,0:T(8,128)S(1)} %shard_map.37.mine), channel_id=1, source_target_pairs={{0,8},{8,0},{16,24},{24,16},{1,9},{9,1},{17,25},{25,17},{2,10},{10... | collective-permute-start | bytes 786440 | tf_op jit(solution)/shard_map/ppermute | solution.py:396
  2.7 6.4 %collective-permute-start.1 = (f32[2,128,128]{2,1,0:T(8,128)S(1)}, f32[2,128,128]{2,1,0:T(8,128)S(1)}, u32[]{:S(2)}, u32[]{:S(2)}) collective-permute-start(f32[2,128,128]{2,1,0:T(8,128)S(1)} %get-tuple-element.16), channel_id=1, source_target_pairs={{0,8},{8,0},{16,24},{24,16},{1,9},{9,1},{17,25},{25,17},{2,10},{10... | collective-permute-start | bytes 393224 | tf_op jit(solution)/shard_map/ppermute | solution.py:400
  9.1 0.1 collective-permute-done.theirs
  9.1 3.1 %collective-permute-done.1.incoming = f32[2,128,128]{2,1,0:T(8,128)S(1)} collective-permute-done((f32[2,128,128]{2,1,0:T(8,128)S(1)}, f32[2,128,128]{2,1,0:T(8,128)S(1)}, u32[]{:S(2)}, u32[]{:S(2)}) %collective-permute-start.1) | collective-permute-done | bytes 131104 | tf_op jit(solution)/shard_map/ppermute | solution.py:400
  12.3 6.3 %shard_map.40 = (f32[2,128,128]{2,1,0:T(8,128)S(1)}, f32[2,128,128]{2,1,0:T(8,128)S(1)}) custom-call(f32[4,128,128]{2,1,0:T(8,128)S(1)} %shard_map.37.mine, f32[2,128,128]{2,1,0:T(8,128)S(1)} %collective-permute-done.1.incoming, f32[2,128,128]{2,1,0:T(8,128)S(1)} %get-tuple-element.17.outer_reduced, f32[2,128,128]{2,1,0:T(8,128)S(1)} %get-tuple-element.18.outer_message), custom_call_target="tpu_custom_call" | custom-call | tf_op jit(solution)/shard_map/pallas_call | solution.py:388
  18.6 0.1 collective-permute-start.2
  18.6 6.6 %collective-permute-done.2.incoming = f32[2,128,128]{2,1,0:T(8,128)S(1)} collective-permute-done((f32[2,128,128]{2,1,0:T(8,128)S(1)}, f32[2,128,128]{2,1,0:T(8,128)S(1)}, u32[]{:S(2)}, u32[]{:S(2)}) %collective-permute-start.2) | collective-permute-done | bytes 131104 | tf_op jit(solution)/shard_map/ppermute | solution.py:403
  25.2 6.5 %shard_map.41 = f32[2,1,128,128]{3,2,1,0:T(8,128)} custom-call(f32[4,128,128]{2,1,0:T(8,128)S(1)} %shard_map.37.mine, f32[4,128,128]{2,1,0:T(8,128)S(1)} %collective-permute-done.theirs, f32[2,128,128]{2,1,0:T(8,128)S(1)} %get-tuple-element.13.end, f32[2,128,128]{2,1,0:T(8,128)S(1)} %get-tuple-element.14.before, f32[2,128,128]{2,1,0:T(8,128)S(1)} %get-tuple-element.15.after, ...), custom_call_target="tpu_custom_call" | custom-call | tf_op jit(solution)/shard_map/pallas_call | solution.py:388
  (2 shorter events, 0.0 us)
Async XLA Ops:
  1.0 8.1 %collective-permute-start = (f32[4,128,128]{2,1,0:T(8,128)S(1)}, f32[4,128,128]{2,1,0:T(8,128)S(1)}, u32[]{:S(2)}, u32[]{:S(2)}) collective-permute-start(f32[4,128,128]{2,1,0:T(8,128)S(1)} %shard_map.37.mine), channel_id=1, source_target_pairs={{0,8},{8,0},{16,24},{24,16},{1,9},{9,1},{17,25},{25,17},{2,10},{10... | collective-permute-start | bytes 786440 | tf_op jit(solution)/shard_map/ppermute | solution.py:396
  2.7 9.6 %collective-permute-start.1 = (f32[2,128,128]{2,1,0:T(8,128)S(1)}, f32[2,128,128]{2,1,0:T(8,128)S(1)}, u32[]{:S(2)}, u32[]{:S(2)}) collective-permute-start(f32[2,128,128]{2,1,0:T(8,128)S(1)} %get-tuple-element.16), channel_id=1, source_target_pairs={{0,8},{8,0},{16,24},{24,16},{1,9},{9,1},{17,25},{25,17},{2,10},{10... | collective-permute-start | bytes 393224 | tf_op jit(solution)/shard_map/ppermute | solution.py:400
  18.6 6.6 %collective-permute-start.2 = (f32[2,128,128]{2,1,0:T(8,128)S(1)}, f32[2,128,128]{2,1,0:T(8,128)S(1)}, u32[]{:S(2)}, u32[]{:S(2)}) collective-permute-start(f32[2,128,128]{2,1,0:T(8,128)S(1)} %get-tuple-element.20), channel_id=1, source_target_pairs={{0,24},{24,0},{8,16},{16,8},{1,25},{25,1},{9,17},{17,9},{2,26},{26... | collective-permute-start | bytes 393224 | tf_op jit(solution)/shard_map/ppermute | solution.py:403

commit v4 on v1

--- a/solution.py
+++ b/solution.py
@@ -93,25 +93,27 @@
             )
             for j in range(TILE)
         ]
+        pivot_re = pivot_im = pivot_scale = None
         for j in range(TILE):
             br, bi = spread[j]
             xr, xi = row(br, j), row(bi, j)
             scale = 1.0 / (xr * xr + xi * xi)
-            qr, qi = xr * scale, -(xi * scale)
             at_row = sub == j
-            ur, ui = times(br, bi, qr, qi)
-            wr, wi = jnp.where(at_row, qr, -ur), jnp.where(at_row, qi, -ui)
+            wr = jnp.where(at_row, 0.0, (br * xr + bi * xi) * scale)
+            wi = jnp.where(at_row, 0.0, (bi * xr - br * xi) * scale)
             for k in range(j + 1, TILE):
                 yr, yi = spread[k]
-                tr, ti = times(wr, wi, row(yr, j), row(yi, j))
-                spread[k] = (jnp.where(at_row, 0.0, yr) + tr, jnp.where(at_row, 0.0, yi) + ti)
+                spread[k] = minus((yr, yi), times(wr, wi, row(yr, j), row(yi, j)))
             at_lane = lane == start + j
-            tr = jnp.where(at_lane, 1.0, row(pr, j))
-            ti = jnp.where(at_lane, 0.0, row(pi, j))
-            tr, ti = times(wr, wi, tr, ti)
-            clear = at_row | at_lane
-            pr = jnp.where(clear, 0.0, pr) + tr
-            pi = jnp.where(clear, 0.0, pi) + ti
+            tr, ti = times(wr, wi, row(pr, j), row(pi, j))
+            pr = jnp.where(at_lane, jnp.where(at_row, 1.0, -wr), pr - tr)
+            pi = jnp.where(at_lane, -wi, pi - ti)
+            if j:
+                xr = jnp.where(at_row, xr, pivot_re)
+                xi = jnp.where(at_row, xi, pivot_im)
+                scale = jnp.where(at_row, scale, pivot_scale)
+            pivot_re, pivot_im, pivot_scale = xr, xi, scale
+        pr, pi = times(pr, pi, pivot_re * pivot_scale, -(pivot_im * pivot_scale))
         ar, ai = re[...], im[...]
 
         def padded(value, start=start, stop=stop):
@@ -219,8 +221,7 @@
             out[part, 0] = value[part]
 
 
-def on_device(onsite, hopping, coupling):
-    assert onsite.shape[1] == 1
+def chain_of_slabs(onsite, hopping, coupling):
     size = onsite.shape[-1]
     pair = jax.ShapeDtypeStruct((2, size, size), jnp.float32)
     scratch = [pltpu.VMEM((size, size), jnp.float32)] * 2
@@ -263,6 +264,182 @@
         incoming = lax.ppermute(result[:, 0], "space", outward)
         result = call(recede_kernel, True, 5, 0)(place, full, green, incoming, before, after)
     return result
+
+
+def choose(condition, former, latter):
+    return jnp.where(condition, former[0], latter[0]), jnp.where(condition, former[1], latter[1])
+
+
+def whereabouts():
+    position = lax.axis_index("space")
+    return position < 2, (position == 0) | (position == 3)
+
+
+def slab_kernel(onsite, hopping, coupling, slab):
+    size = hopping.shape[-1]
+    diagonal = lax.broadcasted_iota(jnp.int32, (size, size), 0) == lax.broadcasted_iota(jnp.int32, (size, size), 1)
+    for part in range(2):
+        slab[part] = jnp.where(diagonal, jnp.broadcast_to(onsite[part], (size, size)), 0.0) - hopping[part, 0]
+        slab[2 + part] = coupling[part, 0]
+
+
+def end_kernel(slab, own, link_adj, message, before, re, im):
+    is_left, is_outer = whereabouts()
+    link = slab.at[pl.ds(2, 2)]
+    store(own, load(slab))
+    store(link_adj, adjoint(load(link)))
+
+    @pl.when(is_outer)
+    def _():
+        @pl.when(is_left)
+        def _():
+            pr, pi = complex_product(load(link_adj), load(link), dot_halves)
+            own[0] = own[0] - pi
+            own[1] = own[1] + pr
+
+        green = inverse(load(own), re, im)
+        store(own, green)
+        store(message, green)
+
+        @pl.when(jnp.logical_not(is_left))
+        def _():
+            store(before, complex_product(load(own), load(link_adj)))
+            store(message, complex_product(load(link), load(before), dot_halves))
+
+
+def send_half(is_left, middle, middle_adj, green, message):
+    store(message, green)
+
+    @pl.when(jnp.logical_not(is_left))
+    def _():
+        inside = complex_product(load(message), load(middle_adj), dot_halves)
+        store(message, complex_product(load(middle), inside, dot_halves))
+
+
+def outer_kernel(inner, own, sigma, before, reduced, theirs_adj, before_out, message, re, im):
+    is_left, is_outer = whereabouts()
+
+    @pl.when(is_outer)
+    def _():
+        theirs = inner.at[pl.ds(2, 2)]
+        store(theirs_adj, adjoint(load(theirs)))
+        store(reduced, load(sigma))
+        store(before_out, load(before))
+
+        @pl.when(is_left)
+        def _():
+            store(before_out, complex_product(load(own), load(theirs)))
+            store(reduced, complex_product(load(theirs_adj), load(before_out), dot_halves))
+
+        value = minus(load(inner), load(reduced))
+        store(reduced, value)
+        send_half(is_left, theirs, theirs_adj, inverse(value, re, im), message)
+
+
+def inner_kernel(slab, link_adj, incoming, outer_reduced, outer_message, reduced, message, re, im):
+    is_left, is_outer = whereabouts()
+    link = slab.at[pl.ds(2, 2)]
+
+    @pl.when(is_outer)
+    def _():
+        store(reduced, load(outer_reduced))
+        store(message, load(outer_message))
+
+    @pl.when(jnp.logical_not(is_outer))
+    def _():
+        store(reduced, load(incoming))
+
+        @pl.when(is_left)
+        def _():
+            inside = complex_product(load(incoming), load(link), dot_halves)
+            store(reduced, complex_product(load(link_adj), inside, dot_halves))
+
+        value = minus(load(slab), load(reduced))
+        store(reduced, value)
+        send_half(is_left, link, link_adj, inverse(value, re, im), message)
+
+
+def factor_kernel(own, slab, theirs_adj, after):
+    is_left, is_outer = whereabouts()
+
+    @pl.when(is_outer)
+    def _():
+        store(after, complex_product(choose(is_left, load(theirs_adj), load(slab.at[pl.ds(2, 2)])), load(own)))
+
+
+def close_kernel(
+    own, slab, link_adj, inner, theirs_adj, before, after, reduced, incoming, out, full, re, im
+):
+    is_left, is_outer = whereabouts()
+    store(full, load(incoming))
+
+    @pl.when(jnp.logical_not(is_left))
+    def _():
+        middle = choose(is_outer, load(inner.at[pl.ds(2, 2)]), load(slab.at[pl.ds(2, 2)]))
+        middle_adj = choose(is_outer, load(theirs_adj), load(link_adj))
+        inside = complex_product(load(incoming), middle, dot_halves)
+        store(full, complex_product(middle_adj, inside, dot_halves))
+
+    green = inverse(minus(load(reduced), load(full)), re, im, refine=True)
+
+    @pl.when(jnp.logical_not(is_outer))
+    def _():
+        out[0, 0] = green[0]
+        out[1, 0] = green[1]
+
+    @pl.when(is_outer)
+    def _():
+        store(full, green)
+        change = complex_product(complex_product(load(before), load(full)), load(after))
+        out[0, 0] = own[0] + change[0]
+        out[1, 0] = own[1] + change[1]
+
+
+def four_slabs(onsite, hopping, coupling):
+    size = onsite.shape[-1]
+    scratch = [pltpu.VMEM((size, size), jnp.float32)] * 2
+    within_halves = [(0, 1), (1, 0), (2, 3), (3, 2)]
+    across = [(0, 3), (3, 0), (1, 2), (2, 1)]
+
+    def on_chip(value):
+        return pltpu.with_memory_space_constraint(value, pltpu.VMEM)
+
+    def call(kernel, outputs, scratch_shapes, *operands):
+        vmem = pl.BlockSpec(memory_space=pltpu.VMEM)
+        results = pl.pallas_call(
+            kernel,
+            out_shape=[pltpu.VMEM((planes, size, size), jnp.float32) for planes in outputs],
+            in_specs=[vmem] * len(operands),
+            scratch_shapes=scratch_shapes,
+        )(*operands)
+        return [on_chip(value) for value in results]
+
+    def move(value, pairs):
+        return on_chip(lax.ppermute(value, "space", pairs))
+
+    slab = call(slab_kernel, [4], [], onsite, hopping, coupling)[0]
+    inner = move(slab, within_halves)
+    own, link_adj, message, before = call(end_kernel, [2] * 4, scratch, slab)
+    incoming = move(message, within_halves)
+    reduced, theirs_adj, before, message = call(outer_kernel, [2] * 4, scratch, inner, own, message, before)
+    reduced, message = call(inner_kernel, [2] * 2, scratch, slab, link_adj, incoming, reduced, message)
+    incoming = move(message, across)
+    late_own, _ = lax.optimization_barrier((own, message))
+    after = call(factor_kernel, [2], [], on_chip(late_own), slab, theirs_adj)[0]
+    vmem = pl.BlockSpec(memory_space=pltpu.VMEM)
+    return pl.pallas_call(
+        close_kernel,
+        out_shape=jax.ShapeDtypeStruct(hopping.shape, jnp.float32),
+        in_specs=[vmem] * 9,
+        scratch_shapes=[pltpu.VMEM((2, size, size), jnp.float32)] + scratch,
+    )(own, slab, link_adj, inner, theirs_adj, before, after, reduced, incoming)
+
+
+def on_device(onsite, hopping, coupling):
+    assert onsite.shape[1] == 1
+    if lax.axis_size("space") == 4:
+        return four_slabs(onsite, hopping, coupling)
+    return chain_of_slabs(onsite, hopping, coupling)
 
 
 def solution(mesh):

time: 51.1 us -> 29.5 us (0.58)
  waiting for transfers between devices: 17.7 us -> 4.57 us
  Pallas kernels: 21.4 us -> 17.2 us
  local copies, waits for them, and re-layouts: 2.57 us -> 0 us
  starting transfers between devices: 8.48 us -> 7.17 us
  other arithmetic: 0.56 us -> 0 us
    ppermute x4 -> x3, waiting for transfers between devices: 17.7 us -> 4.57 us  [move(): return on_chip(lax.ppermute(value, 'space', pairs))]
    pallas_call x5 -> x6, Pallas kernels: 21.4 us -> 17.2 us  [the longest x5 10.9 us: call(): pl.pallas_call(kernel, out_shape=[pltpu.VMEM((planes, size, size), jnp.fl...]
    unnamed x8 -> x0, local copies, waits for them, and re-layouts: 2.57 us -> none
    ppermute x4 -> x3, starting transfers between devices: 8.48 us -> 7.17 us  [move(): return on_chip(lax.ppermute(value, 'space', pairs))]
    another operation x1 -> x0, other arithmetic: 0.56 us -> none  [on_device(): jnp.stack([position, is_left.astype(jnp.int32), is_middle.astype(jnp.int3...]
  transfers between devices with their start and end apart: 4 -> 3, of which waited for: 2 -> 2; matrix products, arithmetic and copies ran while one was open for 1% -> 0% of each run, Pallas kernels for 18% -> 34%
where the time goes in v4:
time: 29.5 us; the launch traced here: 29 us
  Pallas kernels  17.2 us (58%)
  starting transfers between devices  7.17 us (24%)
  waiting for transfers between devices  4.57 us (15%)
    pallas_call x5, Pallas kernels, call(): pl.pallas_call(kernel, out_shape=[pltpu.VMEM((planes, size, size), jnp.fl...  10.9 us
    ppermute x3, starting transfers between devices, move(): return on_chip(lax.ppermute(value, 'space', pairs))  7.17 us
    pallas_call x1, Pallas kernels, four_slabs(): pl.pallas_call(close_kernel, out_shape=jax.ShapeDtypeStruct(hopping.shape...  6.32 us
    ppermute x3, waiting for transfers between devices, move(): return on_chip(lax.ppermute(value, 'space', pairs))  4.57 us
  transfers between devices with their start and end apart: 3, of which 2 were waited for; matrix products, arithmetic and copies ran while one was open for 0% of the time, Pallas kernels for 34%

profile of v4, /device:TPU:0, one launch (start us, length us, event | category | flops | bytes accessed | tf_op | source)
XLA Modules:
  0.0 29.0 jit_solution(7874170367518714619)
XLA Ops:
  0.0 1.0 %shard_map.37.slab = f32[4,128,128]{2,1,0:T(8,128)S(1)} custom-call(f32[2,1,128]{2,1,0:T(1,128)} %onsite.1, f32[2,1,128,128]{3,2,1,0:T(8,128)} %hopping.1, f32[2,1,128,128]{3,2,1,0:T(8,128)} %coupling.1), custom_call_target="tpu_custom_call" | custom-call | tf_op jit(solution)/shard_map/pallas_call | solution.py:409
  1.0 3.1 %collective-permute-start = (f32[4,128,128]{2,1,0:T(8,128)S(1)}, f32[4,128,128]{2,1,0:T(8,128)S(1)}, u32[]{:S(2)}, u32[]{:S(2)}) collective-permute-start(f32[4,128,128]{2,1,0:T(8,128)S(1)} %shard_map.37.slab), channel_id=1, source_target_pairs={{0,8},{8,0},{16,24},{24,16},{1,9},{9,1},{17,25},{25,17},{2,10},{10... | collective-permute-start | bytes 786440 | tf_op jit(solution)/shard_map/ppermute | solution.py:418
  4.1 4.6 %shard_map.38 = (f32[2,128,128]{2,1,0:T(8,128)S(1)}, f32[2,128,128]{2,1,0:T(8,128)S(1)}, f32[2,128,128]{2,1,0:T(8,128)S(1)}, f32[2,128,128]{2,1,0:T(8,128)S(1)}) custom-call(f32[4,128,128]{2,1,0:T(8,128)S(1)} %shard_map.37.slab), custom_call_target="tpu_custom_call" | custom-call | tf_op jit(solution)/shard_map/pallas_call | solution.py:409
  8.7 0.1 collective-permute-start.1
  8.8 1.8 %collective-permute-done.inner = f32[4,128,128]{2,1,0:T(8,128)S(1)} collective-permute-done((f32[4,128,128]{2,1,0:T(8,128)S(1)}, f32[4,128,128]{2,1,0:T(8,128)S(1)}, u32[]{:S(2)}, u32[]{:S(2)}) %collective-permute-start) | collective-permute-done | bytes 262176 | tf_op jit(solution)/shard_map/ppermute | solution.py:418
  10.6 4.9 %shard_map.39 = (f32[2,128,128]{2,1,0:T(8,128)S(1)}, f32[2,128,128]{2,1,0:T(8,128)S(1)}, f32[2,128,128]{2,1,0:T(8,128)S(1)}, f32[2,128,128]{2,1,0:T(8,128)S(1)}) custom-call(f32[4,128,128]{2,1,0:T(8,128)S(1)} %collective-permute-done.inner, f32[2,128,128]{2,1,0:T(8,128)S(1)} %get-tuple-element.25.own, f32[2,128,128]{2,1,0:T(8,128)S(1)} %get-tuple-element.18.sigma, ...), custom_call_target="tpu_custom_call" | custom-call | tf_op jit(solution)/shard_map/pallas_call | solution.py:409
  15.6 0.0 collective-permute-done.1.incoming
  15.6 4.0 %collective-permute-start.2 = (f32[2,128,128]{2,1,0:T(8,128)S(1)}, f32[2,128,128]{2,1,0:T(8,128)S(1)}, u32[]{:S(2)}, u32[]{:S(2)}) collective-permute-start(f32[2,128,128]{2,1,0:T(8,128)S(1)} %get-tuple-element.24), channel_id=1, source_target_pairs={{0,24},{24,0},{8,16},{16,8},{1,25},{25,1},{9,17},{17,9},{2,26},{26... | collective-permute-start | bytes 393224 | tf_op jit(solution)/shard_map/ppermute | solution.py:418
  19.6 0.3 shard_map.41.after
  19.9 2.8 %collective-permute-done.2.incoming = f32[2,128,128]{2,1,0:T(8,128)S(1)} collective-permute-done((f32[2,128,128]{2,1,0:T(8,128)S(1)}, f32[2,128,128]{2,1,0:T(8,128)S(1)}, u32[]{:S(2)}, u32[]{:S(2)}) %collective-permute-start.2) | collective-permute-done | bytes 131104 | tf_op jit(solution)/shard_map/ppermute | solution.py:418
  22.7 6.3 %shard_map.42 = f32[2,1,128,128]{3,2,1,0:T(8,128)} custom-call(f32[2,128,128]{2,1,0:T(8,128)S(1)} %get-tuple-element.25.own, f32[4,128,128]{2,1,0:T(8,128)S(1)} %shard_map.37.slab, f32[2,128,128]{2,1,0:T(8,128)S(1)} %get-tuple-element.17.link_adj, f32[4,128,128]{2,1,0:T(8,128)S(1)} %collective-permute-done.inner, ...), custom_call_target="tpu_custom_call" | custom-call | tf_op jit(solution)/shard_map/pallas_call | solution.py:430
  (1 shorter events, 0.0 us)
Async XLA Ops:
  1.0 9.6 %collective-permute-start = (f32[4,128,128]{2,1,0:T(8,128)S(1)}, f32[4,128,128]{2,1,0:T(8,128)S(1)}, u32[]{:S(2)}, u32[]{:S(2)}) collective-permute-start(f32[4,128,128]{2,1,0:T(8,128)S(1)} %shard_map.37.slab), channel_id=1, source_target_pairs={{0,8},{8,0},{16,24},{24,16},{1,9},{9,1},{17,25},{25,17},{2,10},{10... | collective-permute-start | bytes 786440 | tf_op jit(solution)/shard_map/ppermute | solution.py:418
  8.7 6.8 %collective-permute-start.1 = (f32[2,128,128]{2,1,0:T(8,128)S(1)}, f32[2,128,128]{2,1,0:T(8,128)S(1)}, u32[]{:S(2)}, u32[]{:S(2)}) collective-permute-start(f32[2,128,128]{2,1,0:T(8,128)S(1)} %get-tuple-element.18.sigma), channel_id=1, source_target_pairs={{0,8},{8,0},{16,24},{24,16},{1,9},{9,1},{17,25},{25,17},{2,10},{10... | collective-permute-start | bytes 393224 | tf_op jit(solution)/shard_map/ppermute | solution.py:418
  15.6 7.0 %collective-permute-start.2 = (f32[2,128,128]{2,1,0:T(8,128)S(1)}, f32[2,128,128]{2,1,0:T(8,128)S(1)}, u32[]{:S(2)}, u32[]{:S(2)}) collective-permute-start(f32[2,128,128]{2,1,0:T(8,128)S(1)} %get-tuple-element.24), channel_id=1, source_target_pairs={{0,24},{24,0},{8,16},{16,8},{1,25},{25,1},{9,17},{17,9},{2,26},{26... | collective-permute-start | bytes 393224 | tf_op jit(solution)/shard_map/ppermute | solution.py:418

commit v5 on v4

--- a/solution.py
+++ b/solution.py
@@ -137,18 +137,20 @@
         past = (pr, pi)
 
 
+def refined(matrix, estimate):
+    size = estimate[0].shape[0]
+    diagonal = lax.broadcasted_iota(jnp.int32, (size, size), 0) == lax.broadcasted_iota(jnp.int32, (size, size), 1)
+    pr, pi = complex_product(matrix, estimate)
+    rest = jnp.where(diagonal, 1.0, 0.0) - pr, -pi
+    return plus(estimate, complex_product(estimate, rest, dot_halves))
+
+
 def inverse(matrix, re, im, refine=False):
     re[...] = matrix[0]
     im[...] = matrix[1]
     gauss_jordan(re, im)
     result = re[...], im[...]
-    if refine:
-        size = re.shape[0]
-        diagonal = lax.broadcasted_iota(jnp.int32, (size, size), 0) == lax.broadcasted_iota(jnp.int32, (size, size), 1)
-        pr, pi = complex_product(matrix, result)
-        rest = jnp.where(diagonal, 1.0, 0.0) - pr, -pi
-        result = plus(result, complex_product(result, rest, dot_halves))
-    return result
+    return refined(matrix, result) if refine else result
 
 
 def begin_kernel(place, onsite, hopping, coupling, matrix, green, re, im):
@@ -275,15 +277,33 @@
     return position < 2, (position == 0) | (position == 3)
 
 
-def slab_kernel(onsite, hopping, coupling, slab):
+def slab_kernel(onsite, hopping, coupling, slab, parcel):
     size = hopping.shape[-1]
-    diagonal = lax.broadcasted_iota(jnp.int32, (size, size), 0) == lax.broadcasted_iota(jnp.int32, (size, size), 1)
+    row = lax.broadcasted_iota(jnp.int32, (size, size), 0)
+    lane = lax.broadcasted_iota(jnp.int32, (size, size), 1)
     for part in range(2):
-        slab[part] = jnp.where(diagonal, jnp.broadcast_to(onsite[part], (size, size)), 0.0) - hopping[part, 0]
+        spread = jnp.broadcast_to(onsite[part], (size, size))
+        slab[part] = jnp.where(row == lane, spread, 0.0) - hopping[part, 0]
         slab[2 + part] = coupling[part, 0]
-
-
-def end_kernel(slab, own, link_adj, message, before, re, im):
+        parcel[pl.ds(size + TILE + part * size, size), :] = coupling[part, 0]
+    parcel[pl.ds(0, size), :] = jnp.where(row > lane, slab[1], slab[0])
+    parcel[pl.ds(size, TILE), :] = jnp.broadcast_to(onsite[1], (TILE, size))
+
+
+def unpack(parcel, slab):
+    size = parcel.shape[-1]
+    row = lax.broadcasted_iota(jnp.int32, (size, size), 0)
+    lane = lax.broadcasted_iota(jnp.int32, (size, size), 1)
+    both = parcel[pl.ds(0, size), :]
+    turned = both.T
+    diagonal = jnp.broadcast_to(parcel[pl.ds(size, 1), :], (size, size))
+    slab[0] = jnp.where(row > lane, turned, both)
+    slab[1] = jnp.where(row > lane, both, jnp.where(row < lane, -turned, diagonal))
+    for part in range(2):
+        slab[2 + part] = parcel[pl.ds(size + TILE + part * size, size), :]
+
+
+def end_kernel(slab, own, link_adj, message, re, im):
     is_left, is_outer = whereabouts()
     link = slab.at[pl.ds(2, 2)]
     store(own, load(slab))
@@ -303,8 +323,8 @@
 
         @pl.when(jnp.logical_not(is_left))
         def _():
-            store(before, complex_product(load(own), load(link_adj)))
-            store(message, complex_product(load(link), load(before), dot_halves))
+            inside = complex_product(load(own), load(link_adj), dot_halves)
+            store(message, complex_product(load(link), inside, dot_halves))
 
 
 def send_half(is_left, middle, middle_adj, green, message):
@@ -316,20 +336,20 @@
         store(message, complex_product(load(middle), inside, dot_halves))
 
 
-def outer_kernel(inner, own, sigma, before, reduced, theirs_adj, before_out, message, re, im):
+def outer_kernel(parcel, own, sigma, inner, reduced, theirs_adj, message, re, im):
     is_left, is_outer = whereabouts()
 
     @pl.when(is_outer)
     def _():
+        unpack(parcel, inner)
         theirs = inner.at[pl.ds(2, 2)]
         store(theirs_adj, adjoint(load(theirs)))
         store(reduced, load(sigma))
-        store(before_out, load(before))
 
         @pl.when(is_left)
         def _():
-            store(before_out, complex_product(load(own), load(theirs)))
-            store(reduced, complex_product(load(theirs_adj), load(before_out), dot_halves))
+            inside = complex_product(load(own), load(theirs), dot_halves)
+            store(reduced, complex_product(load(theirs_adj), inside, dot_halves))
 
         value = minus(load(inner), load(reduced))
         store(reduced, value)
@@ -359,12 +379,14 @@
         send_half(is_left, link, link_adj, inverse(value, re, im), message)
 
 
-def factor_kernel(own, slab, theirs_adj, after):
+def factor_kernel(own, slab, link_adj, inner, theirs_adj, before, after):
     is_left, is_outer = whereabouts()
 
     @pl.when(is_outer)
     def _():
-        store(after, complex_product(choose(is_left, load(theirs_adj), load(slab.at[pl.ds(2, 2)])), load(own)))
+        link, theirs = load(slab.at[pl.ds(2, 2)]), load(inner.at[pl.ds(2, 2)])
+        store(before, complex_product(load(own), choose(is_left, theirs, load(link_adj))))
+        store(after, complex_product(choose(is_left, load(theirs_adj), link), load(own)))
 
 
 def close_kernel(
@@ -380,7 +402,7 @@
         inside = complex_product(load(incoming), middle, dot_halves)
         store(full, complex_product(middle_adj, inside, dot_halves))
 
-    green = inverse(minus(load(reduced), load(full)), re, im, refine=True)
+    green = inverse(minus(load(reduced), load(full)), re, im)
 
     @pl.when(jnp.logical_not(is_outer))
     def _():
@@ -389,7 +411,8 @@
 
     @pl.when(is_outer)
     def _():
-        store(full, green)
+        value = minus(load(reduced), load(full))
+        store(full, refined(value, (re[...], im[...])))
         change = complex_product(complex_product(load(before), load(full)), load(after))
         out[0, 0] = own[0] + change[0]
         out[1, 0] = own[1] + change[1]
@@ -408,7 +431,7 @@
         vmem = pl.BlockSpec(memory_space=pltpu.VMEM)
         results = pl.pallas_call(
             kernel,
-            out_shape=[pltpu.VMEM((planes, size, size), jnp.float32) for planes in outputs],
+            out_shape=[pltpu.VMEM(shape, jnp.float32) for shape in outputs],
             in_specs=[vmem] * len(operands),
             scratch_shapes=scratch_shapes,
         )(*operands)
@@ -417,15 +440,19 @@
     def move(value, pairs):
         return on_chip(lax.ppermute(value, "space", pairs))
 
-    slab = call(slab_kernel, [4], [], onsite, hopping, coupling)[0]
-    inner = move(slab, within_halves)
-    own, link_adj, message, before = call(end_kernel, [2] * 4, scratch, slab)
+    pair, double = (2, size, size), (4, size, size)
+    parcel_shape = (3 * size + TILE, size)
+    slab, parcel = call(slab_kernel, [double, parcel_shape], [], onsite, hopping, coupling)
+    parcel = move(parcel, within_halves)
+    own, link_adj, message = call(end_kernel, [pair] * 3, scratch, slab)
     incoming = move(message, within_halves)
-    reduced, theirs_adj, before, message = call(outer_kernel, [2] * 4, scratch, inner, own, message, before)
-    reduced, message = call(inner_kernel, [2] * 2, scratch, slab, link_adj, incoming, reduced, message)
+    inner, reduced, theirs_adj, message = call(outer_kernel, [double] + [pair] * 3, scratch, parcel, own, message)
+    reduced, message = call(inner_kernel, [pair] * 2, scratch, slab, link_adj, incoming, reduced, message)
     incoming = move(message, across)
     late_own, _ = lax.optimization_barrier((own, message))
-    after = call(factor_kernel, [2], [], on_chip(late_own), slab, theirs_adj)[0]
+    before, after = call(
+        factor_kernel, [pair] * 2, [], on_chip(late_own), slab, link_adj, inner, theirs_adj
+    )
     vmem = pl.BlockSpec(memory_space=pltpu.VMEM)
     return pl.pallas_call(
         close_kernel,

time: 29.5 us -> 27.7 us (0.939)
  waiting for transfers between devices: 4.57 us -> 2.97 us
    ppermute x3, waiting for transfers between devices: 4.57 us -> 2.97 us  [move(): return on_chip(lax.ppermute(value, 'space', pairs))]
  transfers between devices with their start and end apart: 3 -> 3, of which waited for: 2 -> 2; matrix products, arithmetic and copies ran while one was open for 0% -> 0% of each run, Pallas kernels for 34% -> 36%
where the time goes in v5:
time: 27.7 us; the launch traced here: 27.3 us
  Pallas kernels  17.3 us (62%)
  starting transfers between devices  7.02 us (25%)
  waiting for transfers between devices  2.97 us (11%)
    pallas_call x5, Pallas kernels, call(): pl.pallas_call(kernel, out_shape=[pltpu.VMEM(shape, jnp.float32) for shap...  11 us
    ppermute x3, starting transfers between devices, move(): return on_chip(lax.ppermute(value, 'space', pairs))  7.02 us
    pallas_call x1, Pallas kernels, four_slabs(): pl.pallas_call(close_kernel, out_shape=jax.ShapeDtypeStruct(hopping.shape...  6.3 us
    ppermute x3, waiting for transfers between devices, move(): return on_chip(lax.ppermute(value, 'space', pairs))  2.97 us
  transfers between devices with their start and end apart: 3, of which 2 were waited for; matrix products, arithmetic and copies ran while one was open for 0% of the time, Pallas kernels for 36%

profile of v5, /device:TPU:0, one launch (start us, length us, event | category | flops | bytes accessed | tf_op | source)
XLA Modules:
  0.0 27.3 jit_solution(17553005862005410950)
XLA Ops:
  0.0 1.0 %shard_map.37 = (f32[4,128,128]{2,1,0:T(8,128)S(1)}, f32[392,128]{1,0:T(8,128)S(1)}) custom-call(f32[2,1,128]{2,1,0:T(1,128)} %onsite.1, f32[2,1,128,128]{3,2,1,0:T(8,128)} %hopping.1, f32[2,1,128,128]{3,2,1,0:T(8,128)} %coupling.1), custom_call_target="tpu_custom_call" | custom-call | tf_op jit(solution)/shard_map/pallas_call | solution.py:432
  1.0 3.1 %collective-permute-start = (f32[392,128]{1,0:T(8,128)S(1)}, f32[392,128]{1,0:T(8,128)S(1)}, u32[]{:S(2)}, u32[]{:S(2)}) collective-permute-start(f32[392,128]{1,0:T(8,128)S(1)} %get-tuple-element.22), channel_id=1, source_target_pairs={{0,8},{8,0},{16,24},{24,16},{1,9},{9,1},{17,25},{25,17},{2,10},{10... | collective-permute-start | bytes 602120 | tf_op jit(solution)/shard_map/ppermute | solution.py:441
  4.1 4.6 %shard_map.38 = (f32[2,128,128]{2,1,0:T(8,128)S(1)}, f32[2,128,128]{2,1,0:T(8,128)S(1)}, f32[2,128,128]{2,1,0:T(8,128)S(1)}) custom-call(f32[4,128,128]{2,1,0:T(8,128)S(1)} %get-tuple-element.19.slab), custom_call_target="tpu_custom_call" | custom-call | tf_op jit(solution)/shard_map/pallas_call | solution.py:432
  8.7 0.1 collective-permute-start.1
  8.8 0.3 %collective-permute-done.parcel = f32[392,128]{1,0:T(8,128)S(1)} collective-permute-done((f32[392,128]{1,0:T(8,128)S(1)}, f32[392,128]{1,0:T(8,128)S(1)}, u32[]{:S(2)}, u32[]{:S(2)}) %collective-permute-start) | collective-permute-done | bytes 200736 | tf_op jit(solution)/shard_map/ppermute | solution.py:441
  9.1 4.9 %shard_map.39 = (f32[4,128,128]{2,1,0:T(8,128)S(1)}, f32[2,128,128]{2,1,0:T(8,128)S(1)}, f32[2,128,128]{2,1,0:T(8,128)S(1)}, f32[2,128,128]{2,1,0:T(8,128)S(1)}) custom-call(f32[392,128]{1,0:T(8,128)S(1)} %collective-permute-done.parcel, f32[2,128,128]{2,1,0:T(8,128)S(1)} %get-tuple-element.29.own, f32[2,128,128]{2,1,0:T(8,128)S(1)} %get-tuple-element.23.sigma), custom_call_target="tpu_custom_call" | custom-call | tf_op jit(solution)/shard_map/pallas_call | solution.py:432
  14.0 0.0 collective-permute-done.1.incoming
  14.1 3.8 %collective-permute-start.2 = (f32[2,128,128]{2,1,0:T(8,128)S(1)}, f32[2,128,128]{2,1,0:T(8,128)S(1)}, u32[]{:S(2)}, u32[]{:S(2)}) collective-permute-start(f32[2,128,128]{2,1,0:T(8,128)S(1)} %get-tuple-element.28), channel_id=1, source_target_pairs={{0,24},{24,0},{8,16},{16,8},{1,25},{25,1},{9,17},{17,9},{2,26},{26... | collective-permute-start | bytes 393224 | tf_op jit(solution)/shard_map/ppermute | solution.py:441
  17.9 0.4 %shard_map.41 = (f32[2,128,128]{2,1,0:T(8,128)S(1)}, f32[2,128,128]{2,1,0:T(8,128)S(1)}) custom-call(f32[2,128,128]{2,1,0:T(8,128)S(1)} %get-tuple-element.29.own, f32[4,128,128]{2,1,0:T(8,128)S(1)} %get-tuple-element.19.slab, f32[2,128,128]{2,1,0:T(8,128)S(1)} %get-tuple-element.21.link_adj, f32[4,128,128]{2,1,0:T(8,128)S(1)} %get-tuple-element.24.inner, ...), custom_call_target="tpu_custom_call" | custom-call | tf_op jit(solution)/shard_map/pallas_call | solution.py:432
  18.4 2.7 %collective-permute-done.2.incoming = f32[2,128,128]{2,1,0:T(8,128)S(1)} collective-permute-done((f32[2,128,128]{2,1,0:T(8,128)S(1)}, f32[2,128,128]{2,1,0:T(8,128)S(1)}, u32[]{:S(2)}, u32[]{:S(2)}) %collective-permute-start.2) | collective-permute-done | bytes 131104 | tf_op jit(solution)/shard_map/ppermute | solution.py:441
  21.0 6.3 %shard_map.42 = f32[2,1,128,128]{3,2,1,0:T(8,128)} custom-call(f32[2,128,128]{2,1,0:T(8,128)S(1)} %get-tuple-element.29.own, f32[4,128,128]{2,1,0:T(8,128)S(1)} %get-tuple-element.19.slab, f32[2,128,128]{2,1,0:T(8,128)S(1)} %get-tuple-element.21.link_adj, f32[4,128,128]{2,1,0:T(8,128)S(1)} %get-tuple-element.24.inner, ...), custom_call_target="tpu_custom_call" | custom-call | tf_op jit(solution)/shard_map/pallas_call | solution.py:457
  (1 shorter events, 0.0 us)
Async XLA Ops:
  1.0 8.1 %collective-permute-start = (f32[392,128]{1,0:T(8,128)S(1)}, f32[392,128]{1,0:T(8,128)S(1)}, u32[]{:S(2)}, u32[]{:S(2)}) collective-permute-start(f32[392,128]{1,0:T(8,128)S(1)} %get-tuple-element.22), channel_id=1, source_target_pairs={{0,8},{8,0},{16,24},{24,16},{1,9},{9,1},{17,25},{25,17},{2,10},{10... | collective-permute-start | bytes 602120 | tf_op jit(solution)/shard_map/ppermute | solution.py:441
  8.7 5.3 %collective-permute-start.1 = (f32[2,128,128]{2,1,0:T(8,128)S(1)}, f32[2,128,128]{2,1,0:T(8,128)S(1)}, u32[]{:S(2)}, u32[]{:S(2)}) collective-permute-start(f32[2,128,128]{2,1,0:T(8,128)S(1)} %get-tuple-element.23.sigma), channel_id=1, source_target_pairs={{0,8},{8,0},{16,24},{24,16},{1,9},{9,1},{17,25},{25,17},{2,10},{10... | collective-permute-start | bytes 393224 | tf_op jit(solution)/shard_map/ppermute | solution.py:441
  14.1 6.9 %collective-permute-start.2 = (f32[2,128,128]{2,1,0:T(8,128)S(1)}, f32[2,128,128]{2,1,0:T(8,128)S(1)}, u32[]{:S(2)}, u32[]{:S(2)}) collective-permute-start(f32[2,128,128]{2,1,0:T(8,128)S(1)} %get-tuple-element.28), channel_id=1, source_target_pairs={{0,24},{24,0},{8,16},{16,8},{1,25},{25,1},{9,17},{17,9},{2,26},{26... | collective-permute-start | bytes 393224 | tf_op jit(solution)/shard_map/ppermute | solution.py:441
